TPU v7x, 512 devices: a whole 4x8x8 slice. The times are simulated.
512 devices in a mesh: tm: 16 (over y, core), chan: 32 (over z, x).
Axes of the slice: x: 4, y: 8, z: 8, core: 2. Of those that a mesh axis runs over, the one named last changes fastest.
Arguments:
- strain: float32 [1024, 65536], P('chan', 'tm'), may hold values from -16 to 16
- channel_mask: int32 [1024], P('chan'), may hold values 0 or 1
Outputs:
- cleaned: float32 [1024, 65536], P('chan', 'tm')
All inputs are finite; a program needn't handle non-finite values. No bound on the sum of `channel_mask` on one device may be relied on, other than what follows from the above.
Results may differ from a plain program's by a relative error of at most 0.0003.
Values sent between devices are 32-bit elements; how exact they have to be, the bound alone decides.
A program may use at most 64 MiB of HBM per device.

v0:
```python
import math

import jax
import jax.numpy as jnp
import numpy as np
from jax import lax
from jax.sharding import PartitionSpec as P

RADIUS = 16


low_corner = 0.015
high_corner = 100.0
sample_rate = 500.0
highest = lax.Precision.HIGHEST


def carried_in(value, axis, combine, identity, reverse):
    size, index = (lax.axis_size(axis), lax.axis_index(axis))
    everything = jax.tree.map(lambda part: lax.all_gather(part, axis), value)
    start = jax.tree.map(
        lambda part, zero: jnp.broadcast_to(jnp.asarray(zero, part.dtype), part.shape),
        value,
        identity,
    )

    def lap(k, before):
        at = size - 1 - k if reverse else k
        reached = at > index if reverse else at < index
        new = combine(before, jax.tree.map(lambda part: part[at], everything))
        return jax.tree.map(lambda a, b: jnp.where(reached, a, b), new, before)

    return lax.fori_loop(0, size, lap, start)


def with_halo(value, sides, width):
    for axis, dim in sides:
        size, length = (lax.axis_size(axis), value.shape[dim])
        up = [(i, (i + 1) % size) for i in range(size - 1)]
        down = [(j, i) for i, j in up]
        last = lax.slice_in_dim(value, length - width, length, axis=dim)
        leading = lax.slice_in_dim(value, 0, width, axis=dim)
        before = lax.ppermute(last, axis, up)
        after = lax.ppermute(leading, axis, down)
        value = jnp.concatenate([before, value, after], axis=dim)
    return value


def section(corner, highpass):
    warped = 2.0 * sample_rate * math.tan(math.pi * corner / sample_rate)
    scaled = warped / (2.0 * sample_rate * math.sqrt(2.0))
    numer_real = 1.0 - scaled
    denom_real = 1.0 + scaled
    denom_imag = -scaled
    modulus = denom_real * denom_real + denom_imag * denom_imag
    pole_real = (numer_real * denom_real + scaled * denom_imag) / modulus
    pole_imag = (scaled * denom_real - numer_real * denom_imag) / modulus
    pole_norm = pole_real * pole_real + pole_imag * pole_imag
    zero_place = 1.0 if highpass else -1.0
    section_gain = ((1.0 + zero_place * pole_real) ** 2 + pole_imag * pole_imag) / 4.0
    linear = section_gain * (2.0 * pole_real - 2.0 * zero_place)
    constant = section_gain * (1.0 - pole_norm)
    shrink = 1.0 - math.sqrt(pole_norm)
    first_out = linear / shrink
    second = (constant + pole_real * linear) / (pole_imag * shrink)
    rotation = np.array([[pole_real, -pole_imag], [pole_imag, pole_real]])
    inject = np.array([shrink, 0.0])
    return (rotation, inject, np.array([first_out, second]), section_gain)


def filter_system():
    high_rotation, high_inject, high_out, high_gain = section(low_corner, True)
    low_rotation, low_inject, low_out, low_gain = section(high_corner, False)
    upper_rows = np.concatenate([high_rotation, np.zeros((2, 2))], axis=1)
    lower_rows = np.concatenate([np.outer(low_inject, high_out), low_rotation], axis=1)
    transition = np.concatenate([upper_rows, lower_rows], axis=0)
    driving = np.concatenate([high_inject, low_inject * high_gain])
    readout = np.concatenate([high_out * low_gain, low_out])
    direct = low_gain * high_gain
    return (transition, driving, readout, direct)


def spatial_taps(extent):
    positions = np.arange(-extent, extent + 1)
    window = 0.5 * (1.0 + np.cos(np.pi * positions / (extent + 1)))
    window = window / np.sum(window)
    return np.where(positions == 0, 1.0 - window, -window)


def filter_tables(block_size, number_blocks):
    transition, driving, readout, direct = filter_system()
    step_powers = [np.eye(4)]
    for counter in range(block_size):
        step_powers.append(step_powers[-1] @ transition)
    response = np.array(
        [direct] + [readout @ step_powers[counter] @ driving for counter in range(block_size - 1)]
    )
    lag_table = np.arange(block_size)[None, :] - np.arange(block_size)[:, None]
    toeplitz = np.where(lag_table >= 0, response[np.clip(lag_table, 0, block_size - 1)], 0.0)
    inputs_to_end = np.stack(
        [step_powers[block_size - 1 - counter] @ driving for counter in range(block_size)], axis=1
    )
    state_to_output = np.stack(
        [readout @ step_powers[counter] for counter in range(block_size)], axis=1
    )
    levels = [np.eye(4)]
    for counter in range(number_blocks):
        levels.append(levels[-1] @ step_powers[block_size])
    levels = np.stack(levels)
    distance = np.arange(number_blocks)[:, None] - np.arange(number_blocks)[None, :] - 1
    chain_powers = np.where(
        (distance >= 0)[:, :, None, None], levels[np.clip(distance, 0, number_blocks)], 0.0
    )
    carry_in = levels[:number_blocks]
    tail_powers = levels[np.arange(number_blocks - 1, -1, -1)]
    device_power = levels[number_blocks]
    return tuple(
        (
            jnp.asarray(table, jnp.float32)
            for table in (
                toeplitz,
                inputs_to_end,
                state_to_output,
                chain_powers,
                carry_in,
                tail_powers,
                device_power,
            )
        )
    )


def boundary(device_power, device_end, reverse):

    def combine(earlier, later):
        return (
            jnp.dot(later[0], earlier[0], precision=highest),
            jnp.dot(later[0], earlier[1], precision=highest) + later[1],
        )

    identity = (jnp.eye(4, dtype=jnp.float32), jnp.zeros_like(device_end))
    composed = carried_in((device_power, device_end), "tm", combine, identity, reverse)
    return composed[1]


def local_pass(record, tables, reverse):
    channels, samples = record.shape
    toeplitz, inputs_to_end, state_to_output, chain_powers, carry_in, tail_powers, device_power = (
        tables
    )
    blocks = record.reshape(channels, samples // 128, 128)
    unforced = jnp.einsum("cbm,mk->cbk", blocks, toeplitz, precision=highest)
    block_ends = jnp.einsum("pm,cbm->pcb", inputs_to_end, blocks, precision=highest)
    starts = jnp.einsum("bjpq,qcj->pcb", chain_powers, block_ends, precision=highest)
    device_end = jnp.einsum("jpq,qcj->pc", tail_powers, block_ends, precision=highest)
    entering = boundary(device_power, device_end, reverse)
    starts = starts + jnp.einsum("bpq,qc->pcb", carry_in, entering, precision=highest)
    result = unforced + jnp.einsum("pk,pcb->cbk", state_to_output, starts, precision=highest)
    return result.reshape(channels, samples)


def bandpass(record, tables):
    forward = local_pass(record, tables, False)
    backward = local_pass(jnp.flip(forward, axis=1), tables, True)
    return jnp.flip(backward, axis=1)


def shards(strain, channel_mask):
    channels, samples = strain.shape
    tables = filter_tables(128, samples // 128)
    weighting = channel_mask.astype(jnp.float32)[:, None]
    taps = spatial_taps(RADIUS)
    lag_table = np.arange(channels + 2 * RADIUS)[None, :] - np.arange(channels)[:, None]
    band_matrix = np.where(
        (lag_table >= 0) & (lag_table <= 2 * RADIUS), taps[np.clip(lag_table, 0, 2 * RADIUS)], 0.0
    )
    band_matrix = jnp.asarray(band_matrix, jnp.float32)
    filtered = bandpass(strain, tables) * weighting
    padded = with_halo(filtered, (("chan", 0),), RADIUS)
    return jnp.dot(band_matrix, padded, precision=highest)


def solution(mesh):
    placed = (P("chan", "tm"), P("chan"))
    return jax.shard_map(
        shards, mesh=mesh, in_specs=placed, out_specs=P("chan", "tm"), check_vma=False
    )
```

profile of v0, /device:TPU:256, one launch (start us, length us, event | category | flops | bytes accessed | tf_op | source)
XLA Modules:
  0.0 89.4 jit_solution(2132363767405037528)
XLA Ops:
  0.0 0.7 copy-done.9
  0.7 17.6 %all_gather.21 = f32[16,4,4]{2,1,0:T(4,128)S(1)} all-gather(f32[1,4,4]{2,1,0:T(4,128)S(1)} %copy-done.9), channel_id=1, replica_groups=mesh['tm'=16,'chan'=32] {'tm'}, dimensions={0}, use_global_device_ids=true | all-gather | bytes 1088 | tf_op jit(solution)/shard_map/all_gather | solution.py:20
  18.3 1.1 %copy.23 = f32[4,8,32,128]{3,2,1,0:T(8,128)S(1)} copy(f32[4,8,32,128]{3,1,2,0:T(8,128)} %bitcast.96) | data formatting | bytes 1048576
  19.5 2.1 %fusion.31 = f32[4,32,32]{2,0,1:T(4,128)S(1)} fusion(f32[4,128,1]{1,0,2:T(4,128)S(1)} %copy-done.8, f32[32,32,128]{2,1,0:T(8,128)S(1)} %bitcast.89), kind=kOutput, calls=%fused_computation.46 | convolution fusion | flops 6291456 | bytes 542720 | tf_op jit(solution)/shard_map/pm,cbm->pcb/dot_general | solution.py:153
  21.7 0.6 convolution_bitcast_fusion
  22.3 0.1 convolution_bitcast_fusion.4
  22.6 0.7 convolution_bitcast_fusion.2
  23.3 15.0 %all-gather.2 = f32[16,4,32]{2,1,0:T(4,128)S(1)} all-gather(f32[1,4,32]{2,1,0:T(4,128)S(1)} %convolution_bitcast_fusion.4), channel_id=2, replica_groups=mesh['tm'=16,'chan'=32] {'tm'}, dimensions={0}, use_global_device_ids=true | all-gather | bytes 8704 | tf_op jit(solution)/shard_map/all_gather | solution.py:20
  38.3 2.4 %while.30 = (s32[]{:T(128)}, f32[4,32]{1,0:T(4,128)S(1)}, s32[]{:T(128)}, f32[16,4,4]{2,1,0:T(4,128)S(1)}, f32[16,4,32]{2,1,0:T(4,128)S(1)}, /*index=5*/s32[]{:T(128)}, s32[]{:T(128)}) while((s32[]{:T(128)}, f32[4,32]{1,0:T(4,128)S(1)}, s32[]{:T(128)}, f32[16,4,4]{2,1,0:T(4,128)S(1)}, f32[16,4,32]{2,1,0:T(4,128)S(1)}, ...), condition=%wide.region_1.2_spmd.clone, body=%wide.region_0.1_spmd.clone.sunk | while | flops 6660 | bytes 12391 | solution.py:33
  38.3 0.1 fusion.66
  38.5 0.1 fusion.66
  38.6 0.1 fusion.66
  38.8 0.1 fusion.66
  38.9 0.1 fusion.66
  39.0 0.1 fusion.66
  39.2 0.1 fusion.66
  39.3 0.1 fusion.66
  39.5 0.1 fusion.66
  39.6 0.1 fusion.66
  39.8 0.1 fusion.66
  39.9 0.1 fusion.66
  40.1 0.1 fusion.66
  40.2 0.1 fusion.66
  40.4 0.1 fusion.66
  40.5 0.1 fusion.66
  40.7 0.3 fusion.19
  41.0 0.4 copy-done.7
  41.4 1.0 %convolution_add_fusion.4 = f32[32,32,128]{2,1,0:T(8,128)S(1)} fusion(f32[32,32,128]{2,1,0:T(8,128)S(1)} %convolution_bitcast_fusion, f32[4,128,1]{1,0,2:T(4,128)S(1)} %copy-done.7, f32[4,32,32]{2,1,0:T(8,128)S(1)} %fusion.19), kind=kOutput, calls=%fused_computation.22 | convolution fusion | flops 6422528 | bytes 1067008 | tf_op jit(solution)/shard_map/pk,pcb->cbk/dot_general | solution.py:158
  42.4 0.3 copy.46
  42.7 2.3 %rev.7 = f32[32,4096]{1,0:T(8,128)S(1)} reverse(f32[32,4096]{1,0:T(8,128)S(1)} %bitcast.93), dimensions={1} | reverse | bytes 1048576 | tf_op jit(solution)/shard_map/jit(_flip)/rev | solution.py:164
  45.1 0.1 copy.25
  45.2 2.1 %fusion.33 = f32[4,32,32]{2,0,1:T(4,128)S(1)} fusion(f32[4,128,1]{1,0,2:T(4,128)S(1)} %copy-done.8, f32[32,32,128]{2,1,0:T(8,128)S(1)} %bitcast.87), kind=kOutput, calls=%fused_computation.48 | convolution fusion | flops 6291456 | bytes 542720 | tf_op jit(solution)/shard_map/pm,cbm->pcb/dot_general | solution.py:153
  47.3 0.6 fusion.32
  47.9 0.1 convolution_bitcast_fusion.3
  48.1 0.7 convolution_bitcast_fusion.1
  48.8 15.4 %all-gather.3 = f32[16,4,32]{2,1,0:T(4,128)S(1)} all-gather(f32[1,4,32]{2,1,0:T(4,128)S(1)} %convolution_bitcast_fusion.3), channel_id=3, replica_groups=mesh['tm'=16,'chan'=32] {'tm'}, dimensions={0}, use_global_device_ids=true | all-gather | bytes 8704 | tf_op jit(solution)/shard_map/all_gather | solution.py:20
  64.3 2.4 %while.31 = (s32[]{:T(128)}, f32[4,32]{1,0:T(4,128)S(1)}, s32[]{:T(128)}, f32[16,4,4]{2,1,0:T(4,128)S(1)}, f32[16,4,32]{2,1,0:T(4,128)S(1)}, /*index=5*/s32[]{:T(128)}, s32[]{:T(128)}, s32[]{:T(128)}, s32[]{:T(128)}) while((s32[]{:T(128)}, f32[4,32]{1,0:T(4,128)S(1)}, s32[]{:T(128)}, f32[16,4,4]{2,1,0:T(4,128)S(1)}, ...), condition=%wide.region_3.4_spmd.clone, body=%wide.region_2.3_spmd.clone.sunk | while | flops 6664 | bytes 12453 | solution.py:33
  64.4 0.1 fusion.69
  64.5 0.1 fusion.69
  64.7 0.1 fusion.69
  64.8 0.1 fusion.69
  65.0 0.1 fusion.69
  65.1 0.1 fusion.69
  65.3 0.1 fusion.69
  65.4 0.1 fusion.69
  65.6 0.1 fusion.69
  65.7 0.1 fusion.69
  65.9 0.1 fusion.69
  66.0 0.1 fusion.69
  66.2 0.1 fusion.69
  66.3 0.1 fusion.69
  66.5 0.1 fusion.69
  66.6 0.3 fusion.18
  66.9 1.0 %convolution_add_fusion.3 = f32[32,32,128]{2,1,0:T(8,128)S(1)} fusion(f32[32,32,128]{2,1,0:T(8,128)S(1)} %fusion.32, f32[4,128,1]{1,0,2:T(4,128)S(1)} %copy-done.7, f32[4,32,32]{2,1,0:T(8,128)S(1)} %fusion.18), kind=kOutput, calls=%fused_computation.21 | convolution fusion | flops 6422528 | bytes 1067008 | tf_op jit(solution)/shard_map/pk,pcb->cbk/dot_general | solution.py:158
  68.0 0.3 copy.45
  68.3 2.3 %rev.8 = f32[32,4096]{1,0:T(8,128)S(1)} reverse(f32[32,4096]{1,0:T(8,128)S(1)} %bitcast.95), dimensions={1} | reverse | bytes 1048576 | tf_op jit(solution)/shard_map/jit(_flip)/rev | solution.py:165
  70.6 0.1 broadcast_multiply_fusion
  70.8 3.8 %collective-permute-start.1 = (f32[16,4096]{1,0:T(8,128)S(1)}, f32[16,4096]{1,0:T(8,128)S(1)}, u32[]{:S(2)}, u32[]{:S(2)}) collective-permute-start(f32[16,4096]{1,0:T(8,128)S(1)} %get-tuple-element.290), channel_id=1, source_target_pairs={{1,0},{2,1},{3,2},{4,3},{5,4},{6,5},{7,6},{8,7},{9,8},{10,9},{11,1... | collective-permute-start | bytes 786440 | tf_op jit(solution)/shard_map/ppermute | solution.py:44
  74.6 2.1 %collective-permute-start = (f32[16,4096]{1,0:T(8,128)S(1)}, f32[16,4096]{1,0:T(8,128)S(1)}, u32[]{:S(2)}, u32[]{:S(2)}) collective-permute-start(f32[16,4096]{1,0:T(8,128)S(1)} %get-tuple-element.289), channel_id=1, source_target_pairs={{0,1},{1,2},{2,3},{3,4},{4,5},{5,6},{6,7},{7,8},{8,9},{9,10},{10,1... | collective-permute-start | bytes 786440 | tf_op jit(solution)/shard_map/ppermute | solution.py:43
  76.7 0.6 fusion.34
  77.3 4.0 %collective-permute-done.1 = f32[16,4096]{1,0:T(8,128)S(1)} collective-permute-done((f32[16,4096]{1,0:T(8,128)S(1)}, f32[16,4096]{1,0:T(8,128)S(1)}, u32[]{:S(2)}, u32[]{:S(2)}) %collective-permute-start.1) | collective-permute-done | bytes 262176 | tf_op jit(solution)/shard_map/ppermute | solution.py:44
  81.3 0.6 fusion.35
  81.8 6.3 %collective-permute-done = f32[16,4096]{1,0:T(8,128)S(1)} collective-permute-done((f32[16,4096]{1,0:T(8,128)S(1)}, f32[16,4096]{1,0:T(8,128)S(1)}, u32[]{:S(2)}, u32[]{:S(2)}) %collective-permute-start) | collective-permute-done | bytes 262176 | tf_op jit(solution)/shard_map/ppermute | solution.py:43
  88.1 1.4 %fusion.17 = f32[32,4096]{1,0:T(8,128)} fusion(f32[4096,32]{0,1:T(8,128)S(1)} %fusion.35, f32[4096,32]{0,1:T(8,128)S(1)} %fusion.34, f32[16,4096]{1,0:T(8,128)S(1)} %collective-permute-done, f32[32,16]{1,0:T(8,128)S(1)} %copy-done.4), kind=kOutput, calls=%fused_computation.20 | convolution fusion | flops 25427968 | bytes 1837056 | tf_op jit(solution)/shard_map/dot_general | solution.py:180
  (57 shorter events, 0.7 us)
Async XLA Ops:
  0.0 0.7 copy-start.9
  18.3 1.2 %copy-start.8 = (f32[4,128,1]{1,0,2:T(4,128)S(1)}, f32[4,128,1]{1,0,2:T(4,128)}, u32[]{:S(2)}) copy-start(f32[4,128,1]{1,0,2:T(4,128)} %constant.103) | copy-start | bytes 6148
  19.5 2.1 %copy-start.1 = (f32[128,128,1]{1,0,2:T(8,128)S(1)}, f32[128,128,1]{1,0,2:T(8,128)}, u32[]{:S(2)}) copy-start(f32[128,128,1]{1,0,2:T(8,128)} %constant.102) | copy-start | bytes 196612
  21.6 0.7 copy-start.3
  21.6 1.0 %copy-start = (f32[32,32,4,4]{1,0,3,2:T(8,128)S(1)}, f32[32,32,4,4]{1,0,3,2:T(8,128)}, u32[]{:S(2)}) copy-start(f32[32,32,4,4]{1,0,3,2:T(8,128)} %constant.93.clone) | copy-start | bytes 196612
  38.3 2.4 %copy-start.2 = (f32[32,4,4]{0,2,1:T(4,128)S(1)}, f32[32,4,4]{0,2,1:T(4,128)}, u32[]{:S(2)}) copy-start(f32[32,4,4]{0,2,1:T(4,128)} %constant.94.clone) | copy-start | bytes 6148
  40.7 0.7 copy-start.7
  48.1 0.7 copy-start.10
  70.8 5.9 %copy-start.5 = (f32[32,32]{1,0:T(8,128)S(1)}, f32[32,32]{1,0:T(8,128)}, u32[]{:S(2)}) copy-start(f32[32,32]{1,0:T(8,128)} %constant.100) | copy-start | bytes 12292
  70.8 10.4 %collective-permute-start.1 = (f32[16,4096]{1,0:T(8,128)S(1)}, f32[16,4096]{1,0:T(8,128)S(1)}, u32[]{:S(2)}, u32[]{:S(2)}) collective-permute-start(f32[16,4096]{1,0:T(8,128)S(1)} %get-tuple-element.290), channel_id=1, source_target_pairs={{1,0},{2,1},{3,2},{4,3},{5,4},{6,5},{7,6},{8,7},{9,8},{10,9},{11,1... | collective-permute-start | bytes 786440 | tf_op jit(solution)/shard_map/ppermute | solution.py:44
  74.6 6.7 %copy-start.6 = (f32[32,16]{1,0:T(8,128)S(1)}, f32[32,16]{1,0:T(8,128)}, u32[]{:S(2)}) copy-start(f32[32,16]{1,0:T(8,128)} %constant.101) | copy-start | bytes 6148
  74.6 13.5 %collective-permute-start = (f32[16,4096]{1,0:T(8,128)S(1)}, f32[16,4096]{1,0:T(8,128)S(1)}, u32[]{:S(2)}, u32[]{:S(2)}) collective-permute-start(f32[16,4096]{1,0:T(8,128)S(1)} %get-tuple-element.289), channel_id=1, source_target_pairs={{0,1},{1,2},{2,3},{3,4},{4,5},{5,6},{6,7},{7,8},{8,9},{9,10},{10,1... | collective-permute-start | bytes 786440 | tf_op jit(solution)/shard_map/ppermute | solution.py:43
  77.3 10.8 %copy-start.4 = (f32[32,16]{1,0:T(8,128)S(1)}, f32[32,16]{1,0:T(8,128)}, u32[]{:S(2)}) copy-start(f32[32,16]{1,0:T(8,128)} %constant.99) | copy-start | bytes 6148
where the time goes:
time: 89.8 us; the launch traced here: 89.4 us
  blocking collectives  48.1 us (54%)
  matrix products  16.7 us (19%)
  waiting for transfers between devices  10.2 us (11%)
  local copies, waits for them, and re-layouts  8.18 us (9%)
  starting transfers between devices  5.84 us (7%)
    all_gather x3, blocking collectives, carried_in(): everything = jax.tree.map(lambda part: lax.all_gather(part, axis), value)  48.1 us
    ppermute x1, waiting for transfers between devices, with_halo(): before = lax.ppermute(last, axis, up)  6.25 us
    dot_general x32, matrix products, combine(): jnp.dot(later[0], earlier[1], precision=highest) + later[1]  4.55 us
    dot_general x2, matrix products, local_pass(): jnp.einsum('pm,cbm->pcb', inputs_to_end, blocks, precision=highest)  4.25 us
    ppermute x1, waiting for transfers between devices, with_halo(): after = lax.ppermute(leading, axis, down)  3.97 us
    ppermute x1, starting transfers between devices, with_halo(): after = lax.ppermute(leading, axis, down)  3.75 us
    unnamed x26, local copies, waits for them, and re-layouts  3.32 us
    dot_general x3, matrix products, shards(): return jnp.dot(band_matrix, padded, precision=highest)  2.5 us
  transfers between devices with their start and end apart: 2, of which 2 were waited for; matrix products, arithmetic and copies ran while one was open for 1% of the time, Pallas kernels for 0%

commit v1 on v0

v1 whole, which is shorter than its diff:
```python
import functools
import math

import jax
import jax.numpy as jnp
import ml_dtypes
import numpy as np
from jax import lax
from jax.experimental import pallas as pl
from jax.experimental.pallas import tpu as pltpu
from jax.sharding import PartitionSpec as P

RADIUS = 16
BLOCK = 256
LANES = 128
PIECES = 4

low_corner = 0.015
high_corner = 100.0
sample_rate = 500.0
highest = lax.Precision.HIGHEST
MESH = pl.DeviceIdType.MESH


def section(corner, highpass):
    warped = 2.0 * sample_rate * math.tan(math.pi * corner / sample_rate)
    scaled = warped / (2.0 * sample_rate * math.sqrt(2.0))
    numer_real = 1.0 - scaled
    denom_real = 1.0 + scaled
    denom_imag = -scaled
    modulus = denom_real * denom_real + denom_imag * denom_imag
    pole_real = (numer_real * denom_real + scaled * denom_imag) / modulus
    pole_imag = (scaled * denom_real - numer_real * denom_imag) / modulus
    pole_norm = pole_real * pole_real + pole_imag * pole_imag
    zero_place = 1.0 if highpass else -1.0
    section_gain = ((1.0 + zero_place * pole_real) ** 2 + pole_imag * pole_imag) / 4.0
    linear = section_gain * (2.0 * pole_real - 2.0 * zero_place)
    constant = section_gain * (1.0 - pole_norm)
    shrink = 1.0 - math.sqrt(pole_norm)
    first_out = linear / shrink
    second = (constant + pole_real * linear) / (pole_imag * shrink)
    rotation = np.array([[pole_real, -pole_imag], [pole_imag, pole_real]])
    inject = np.array([shrink, 0.0])
    return (rotation, inject, np.array([first_out, second]), section_gain)


def filter_system():
    high_rotation, high_inject, high_out, high_gain = section(low_corner, True)
    low_rotation, low_inject, low_out, low_gain = section(high_corner, False)
    upper_rows = np.concatenate([high_rotation, np.zeros((2, 2))], axis=1)
    lower_rows = np.concatenate([np.outer(low_inject, high_out), low_rotation], axis=1)
    transition = np.concatenate([upper_rows, lower_rows], axis=0)
    driving = np.concatenate([high_inject, low_inject * high_gain])
    readout = np.concatenate([high_out * low_gain, low_out])
    direct = low_gain * high_gain
    return (transition, driving, readout, direct)


def spatial_taps(extent):
    positions = np.arange(-extent, extent + 1)
    window = 0.5 * (1.0 + np.cos(np.pi * positions / (extent + 1)))
    window = window / np.sum(window)
    return np.where(positions == 0, 1.0 - window, -window)


def chain(count, power, couple):
    powers = [np.eye(4)]
    for _ in range(count):
        powers.append(powers[-1] @ power)
    ahead = np.zeros((count, 4, count, 8))
    behind = np.zeros((count, 4, count, 8))
    for at in range(count):
        for other in range(at):
            ahead[at, :, other, :4] = powers[at - 1 - other]
    for at in range(count):
        for other in range(at + 1, count):
            gives = np.einsum("pq,qjr->pjr", couple, ahead[other])
            gives[:, other, 4:] += np.eye(4)
            behind[at] += np.einsum("pq,qjr->pjr", powers[other - 1 - at], gives)
    inner = np.concatenate([ahead, behind], axis=1)
    outer = np.zeros((count, 8, 8))
    for at in range(count):
        outer[at, :4, :4] = powers[at]
    for at in range(count):
        outer[at, 4:, 4:] = powers[count - 1 - at]
        for other in range(at + 1, count):
            outer[at, 4:, :4] += powers[other - 1 - at] @ couple @ outer[other, :4, :4]
    total = np.zeros((8, count, 8))
    for other in range(count):
        total[:4, other, :4] = powers[count - 1 - other]
        gives = np.einsum("pq,qjr->pjr", couple, ahead[other])
        gives[:, other, 4:] += np.eye(4)
        total[4:] += np.einsum("pq,qjr->pjr", powers[other], gives)
    pull = sum(powers[other] @ couple @ powers[other] for other in range(count))
    return inner, outer, total, powers[count], pull


def split(table):
    high = np.asarray(table, np.float32).astype(ml_dtypes.bfloat16)
    low = (np.asarray(table, np.float64) - high.astype(np.float64)).astype(np.float32)
    return high, low.astype(ml_dtypes.bfloat16)


def thrice(table):
    high, low = split(table)
    return np.concatenate([high, high, low], axis=0)


@functools.lru_cache(maxsize=None)
def filter_tables(blocks, devices):
    transition, driving, readout, direct = filter_system()
    powers = [np.eye(4)]
    for _ in range(BLOCK):
        powers.append(powers[-1] @ transition)
    response = np.array([direct] + [readout @ powers[lag] @ driving for lag in range(BLOCK - 1)])
    lag = np.arange(BLOCK)[:, None] - np.arange(BLOCK)[None, :]
    forward = np.where(lag >= 0, response[np.clip(lag, 0, BLOCK - 1)], 0.0)
    observe = np.stack([readout @ powers[at] for at in range(BLOCK)])
    reach = np.stack([powers[BLOCK - 1 - at] @ driving for at in range(BLOCK)], axis=1)
    both_ways = forward.T @ forward
    gives = np.concatenate([reach, reach[:, ::-1] @ forward], axis=0)
    takes = np.concatenate([forward.T @ observe, observe[::-1]], axis=1)
    couple = reach[:, ::-1] @ observe
    inner, outer, total, power, pull = chain(blocks, powers[BLOCK], couple)
    across = chain(devices, power, pull)[0]
    width = 8 * blocks
    first = thrice(np.tile(gives.T, (1, blocks)))
    main = thrice(np.concatenate([np.tile(gives.T, (1, blocks)), both_ways], axis=1))
    correct = thrice(np.tile(takes.T, (blocks, 1)))
    return (
        first,
        main,
        correct,
        np.asarray(inner.reshape(width, width).T, np.float32),
        np.asarray(total.reshape(8, width), np.float32),
        np.asarray(outer.reshape(width, 8).T, np.float32),
        np.asarray(across.reshape(devices, 8, devices * 8), np.float32),
    )


@functools.lru_cache(maxsize=None)
def space_tables(channels):
    taps = spatial_taps(RADIUS)

    def band(sources):
        lag = np.asarray(sources)[None, :] - np.arange(channels)[:, None] + RADIUS
        inside = (lag >= 0) & (lag <= 2 * RADIUS)
        return np.where(inside, taps[np.clip(lag, 0, 2 * RADIUS)], 0.0)

    own = band(np.arange(channels))
    edge = np.concatenate(
        [band(np.arange(-RADIUS, 0)), band(np.arange(channels, channels + RADIUS))], axis=1
    )
    parts = []
    for table in (edge, own):
        high, low = split(table)
        parts += [high, low, high]
    states = np.zeros((channels, 3 * LANES))
    states[:, :channels] = own
    states[:, LANES : LANES + channels] = band(np.arange(-channels, 0))
    states[:, 2 * LANES : 2 * LANES + channels] = band(np.arange(channels, 2 * channels))
    return np.concatenate(parts, axis=1), np.asarray(states, np.float32)


def halves(value):
    high = value.astype(jnp.bfloat16)
    return high, (value - high.astype(jnp.float32)).astype(jnp.bfloat16)


def kernel(
    devices,
    groups,
    x_hbm,
    mask_hbm,
    first_hbm,
    main_hbm,
    correct_hbm,
    inner_hbm,
    total_hbm,
    outer_hbm,
    across_hbm,
    space_hbm,
    states_hbm,
    out_hbm,
    x,
    mask,
    first,
    main,
    correct,
    inner,
    total,
    outer,
    across,
    space,
    states,
    halo,
    ends,
    entering,
    plain,
    result,
    load_sem,
    end_send,
    end_recv,
    near_send,
    near_recv,
    halo_send,
    halo_recv,
    out_sem,
):
    channels, samples = x.shape
    blocks = samples // BLOCK
    width = 8 * blocks
    row, column = lax.axis_index("tm"), lax.axis_index("chan")
    below, above = lax.rem(column + groups - 1, groups), lax.rem(column + 1, groups)

    loads = []
    for index, (source, target) in enumerate(
        (
            (mask_hbm, mask),
            (x_hbm, x),
            (first_hbm, first),
            (total_hbm, total),
            (across_hbm.at[row], across),
            (space_hbm, space),
            (states_hbm, states),
            (outer_hbm, outer),
            (inner_hbm, inner),
            (main_hbm, main),
            (correct_hbm, correct),
        )
    ):
        copy = pltpu.make_async_copy(source, target, load_sem.at[index])
        copy.start()
        loads.append(copy)

    barrier = pltpu.get_barrier_semaphore()
    for side in (below, above):
        pl.semaphore_signal(barrier, inc=1, device_id=(row, side), device_id_type=MESH)
    for step in range(1, devices):
        peer = lax.rem(row + step, devices)
        pl.semaphore_signal(barrier, inc=1, device_id=(peer, column), device_id_type=MESH)

    loads[0].wait()
    here = lax.broadcasted_iota(jnp.int32, (channels, channels), 0)
    there = lax.broadcasted_iota(jnp.int32, (channels, channels), 1)
    live = jnp.where(here == there, mask[...].astype(jnp.float32), 0.0)
    live = jnp.sum(live, axis=1, keepdims=True)
    loads[1].wait()
    x[...] = x[...] * live

    pl.semaphore_wait(barrier, devices + 1)

    length = samples // PIECES
    pieces = []
    for piece in range(PIECES):
        span = pl.ds(piece * length, length)
        pair = []
        for way, (side, source, target) in enumerate(
            ((above, channels - RADIUS, 0), (below, 0, RADIUS))
        ):
            copy = pltpu.make_async_remote_copy(
                src_ref=x.at[pl.ds(source, RADIUS), span],
                dst_ref=halo.at[pl.ds(target, RADIUS), span],
                send_sem=halo_send.at[way, piece],
                recv_sem=halo_recv.at[way, piece],
                device_id=(row, side),
                device_id_type=MESH,
            )
            copy.start()
            pair.append(copy)
        pieces.append(pair)

    slot = lax.broadcasted_iota(jnp.int32, (channels, width), 1) // 8

    def stacked(value):
        return jnp.concatenate(
            [value[:, k * BLOCK : (k + 1) * BLOCK] for k in range(value.shape[1] // BLOCK)], axis=0
        )

    def gathered(value, start):
        kept = [
            jnp.where(slot == start + k, value[k * channels : (k + 1) * channels], 0.0)
            for k in range(value.shape[0] // channels)
        ]
        return functools.reduce(jnp.add, kept)

    x_high, x_low = halves(x[...])
    s_high, s_low = stacked(x_high), stacked(x_low)
    loads[2].wait()
    loads[3].wait()
    given = gathered(
        jnp.dot(
            jnp.concatenate([s_high, s_low, s_high], axis=1),
            first[...],
            preferred_element_type=jnp.float32,
        ),
        0,
    )
    nt = (((1,), (1,)), ((), ()))
    mine = lax.dot_general(
        total[...], given, nt, precision=highest, preferred_element_type=jnp.float32
    )
    ends[row] = jnp.concatenate([mine, jnp.zeros((8, LANES - channels), jnp.float32)], axis=1)

    def end_copy(to, slot_index):
        return pltpu.make_async_remote_copy(
            src_ref=ends.at[slot_index],
            dst_ref=ends.at[slot_index],
            send_sem=end_send.at[to],
            recv_sem=end_recv.at[slot_index],
            device_id=(to, column),
            device_id_type=MESH,
        )

    sent = []
    for step in range(1, devices):
        copy = end_copy(lax.rem(row + step, devices), row)
        copy.start()
        sent.append(copy)
    for load in loads[4:]:
        load.wait()

    for step in range(1, devices):
        end_copy(row, lax.rem(row + step, devices)).wait_recv()
    entering[0] = jnp.dot(
        across[...],
        ends[...].reshape(devices * 8, LANES),
        precision=highest,
        preferred_element_type=jnp.float32,
    )
    near = []
    for way, side in enumerate((above, below)):
        copy = pltpu.make_async_remote_copy(
            src_ref=entering.at[0],
            dst_ref=entering.at[1 + way],
            send_sem=near_send.at[way],
            recv_sem=near_recv.at[way],
            device_id=(row, side),
            device_id_type=MESH,
        )
        copy.start()
        near.append(copy)

    has_below = jnp.where(column > 0, 1.0, 0.0).astype(jnp.float32)
    has_above = jnp.where(column < groups - 1, 1.0, 0.0).astype(jnp.float32)
    lane = lax.broadcasted_iota(jnp.int32, (channels, 6 * 2 * RADIUS), 1)
    part = lax.rem(lane, 2 * RADIUS)
    keep = jnp.where(lane >= 3 * 2 * RADIUS, 1.0, jnp.where(part < RADIUS, has_below, has_above))
    band = (space[...].astype(jnp.float32) * keep).astype(jnp.bfloat16)

    collected = jnp.zeros((channels, width), jnp.float32)
    per = length // BLOCK
    for piece in range(PIECES):
        for copy in pieces[piece]:
            copy.wait_recv()
        low, high = piece * length, (piece + 1) * length
        h_high, h_low = halves(halo[:, low:high])
        both = jnp.concatenate(
            [h_high, h_high, h_low, x_high[:, low:high], x_high[:, low:high], x_low[:, low:high]],
            axis=0,
        )
        mixed = jnp.dot(band, both, preferred_element_type=jnp.float32)
        m_high, m_low = halves(stacked(mixed))
        answer = jnp.dot(
            jnp.concatenate([m_high, m_low, m_high], axis=1),
            main[...],
            preferred_element_type=jnp.float32,
        )
        collected = collected + gathered(answer[:, :width], piece * per)
        plain[pl.ds(piece * per * channels, per * channels), :] = answer[:, width:]

    for copy in near:
        copy.wait_recv()
    lane = lax.broadcasted_iota(jnp.int32, (channels, 3 * LANES), 1)
    keep = jnp.where(
        lane < LANES, 1.0, jnp.where(lane < 2 * LANES, has_below, has_above)
    )
    outside = lax.dot_general(
        states[...] * keep,
        jnp.concatenate([entering[0], entering[1], entering[2]], axis=1),
        nt,
        precision=highest,
        preferred_element_type=jnp.float32,
    )
    taken = jnp.dot(
        collected, inner[...], precision=highest, preferred_element_type=jnp.float32
    ) + jnp.dot(outside, outer[...], precision=highest, preferred_element_type=jnp.float32)
    t_high, t_low = halves(taken)
    writes = []
    for piece in range(PIECES):
        rows = []
        for k in range(piece * per, (piece + 1) * per):
            chosen = slot == k
            k_high = jnp.where(chosen, t_high, jnp.zeros_like(t_high))
            k_low = jnp.where(chosen, t_low, jnp.zeros_like(t_low))
            rows.append(jnp.concatenate([k_high, k_low, k_high], axis=1))
        fixed = plain[pl.ds(piece * per * channels, per * channels), :] + jnp.dot(
            jnp.concatenate(rows, axis=0), correct[...], preferred_element_type=jnp.float32
        )
        for k in range(per):
            at = piece * length + k * BLOCK
            result[:, at : at + BLOCK] = fixed[k * channels : (k + 1) * channels]
        span = pl.ds(piece * length, length)
        copy = pltpu.make_async_copy(result.at[:, span], out_hbm.at[:, span], out_sem.at[piece])
        copy.start()
        writes.append(copy)

    for copy in sent + near + [copy for pair in pieces for copy in pair]:
        copy.wait_send()
    for copy in writes:
        copy.wait()


def shards(devices, groups, strain, channel_mask):
    channels, samples = strain.shape
    tables = filter_tables(samples // BLOCK, devices) + space_tables(channels)
    tables = [jnp.asarray(table) for table in tables]
    f32 = jnp.float32
    held = [pltpu.VMEM(table.shape, table.dtype) for table in tables]
    held[6] = pltpu.VMEM(tables[6].shape[1:], f32)
    return pl.pallas_call(
        functools.partial(kernel, devices, groups),
        out_shape=jax.ShapeDtypeStruct((channels, samples), f32),
        in_specs=[pl.BlockSpec(memory_space=pltpu.HBM)] * (2 + len(tables)),
        out_specs=pl.BlockSpec(memory_space=pl.ANY),
        scratch_shapes=[
            pltpu.VMEM((channels, samples), f32),
            pltpu.VMEM((1, channels), jnp.int32),
            *held,
            pltpu.VMEM((2 * RADIUS, samples), f32),
            pltpu.VMEM((devices, 8, LANES), f32),
            pltpu.VMEM((3, 8, LANES), f32),
            pltpu.VMEM((channels * samples // BLOCK, BLOCK), f32),
            pltpu.VMEM((channels, samples), f32),
            pltpu.SemaphoreType.DMA((2 + len(tables),)),
            pltpu.SemaphoreType.DMA((devices,)),
            pltpu.SemaphoreType.DMA((devices,)),
            pltpu.SemaphoreType.DMA((2,)),
            pltpu.SemaphoreType.DMA((2,)),
            pltpu.SemaphoreType.DMA((2, PIECES)),
            pltpu.SemaphoreType.DMA((2, PIECES)),
            pltpu.SemaphoreType.DMA((PIECES,)),
        ],
        compiler_params=pltpu.CompilerParams(
            collective_id=0, has_side_effects=True, vmem_limit_bytes=40 * 1024 * 1024
        ),
        name="bandpass",
    )(
        *[
            pltpu.with_memory_space_constraint(value, pltpu.HBM)
            for value in (strain, channel_mask.reshape(1, channels), *tables)
        ]
    )


def solution(mesh):
    placed = (P("chan", "tm"), P("chan"))
    sizes = dict(zip(mesh.axis_names, mesh.devices.shape))
    return jax.shard_map(
        functools.partial(shards, sizes["tm"], sizes["chan"]),
        mesh=mesh,
        in_specs=placed,
        out_specs=P("chan", "tm"),
        check_vma=False,
    )
```

time: 89.8 us -> 28.6 us (0.32)
  the two profiles are of different devices: /device:TPU:256 before, /device:TPU:1 now
where the time goes in v1:
time: 28.6 us; the launch traced here: 28.4 us
  Pallas kernels  27.6 us (97%)
  local copies, waits for them, and re-layouts  0.8 us (3%)
    pallas_call x1, Pallas kernels, shards(): pl.pallas_call(functools.partial(kernel, devices, groups), out_shape=jax....  27.6 us
    unnamed x1, local copies, waits for them, and re-layouts  0.8 us

profile of v1, /device:TPU:1, one launch (start us, length us, event | category | flops | bytes accessed | tf_op | source)
XLA Modules:
  0.0 28.4 jit_solution(7461199433775834751)
XLA Ops:
  0.0 27.6 %bandpass.1 = f32[32,4096]{1,0:T(8,128)S(1)} custom-call(f32[32,4096]{1,0:T(8,128)} %x_hbm.1, s32[1,32]{1,0:T(1,128)} %bitcast.1, bf16[768,128]{1,0:T(8,128)(2,1)} %constant.18.clone.first_hbm, bf16[768,384]{1,0:T(8,128)(2,1)} %constant.19.clone.main_hbm, bf16[384,256]{1,0:T(8,128)(2,1)} %constant.20.clone.correct_hbm, f32[128,128]{1,0:T(8,128)} %constant.21.clone.inner_hbm, ...), custom_call_target="tpu_custom_call" | custom-call | tf_op jit(solution)/shard_map/bandpass/pallas_call | solution.py:421
  27.6 0.8 %copy.13 = f32[32,4096]{1,0:T(8,128)} copy(f32[32,4096]{1,0:T(8,128)S(1)} %bandpass.1) | data formatting | bytes 1048576

commit v2 on v1

v2 whole, which is shorter than its diff:
```python
import functools
import math

import jax
import jax.numpy as jnp
import ml_dtypes
import numpy as np
from jax import lax
from jax.experimental import pallas as pl
from jax.experimental.pallas import tpu as pltpu
from jax.sharding import PartitionSpec as P

RADIUS = 16
BLOCK = 256
LANES = 128
PIECES = 4
EARLY = 2

low_corner = 0.015
high_corner = 100.0
sample_rate = 500.0
highest = lax.Precision.HIGHEST
MESH = pl.DeviceIdType.MESH


def section(corner, highpass):
    warped = 2.0 * sample_rate * math.tan(math.pi * corner / sample_rate)
    scaled = warped / (2.0 * sample_rate * math.sqrt(2.0))
    numer_real = 1.0 - scaled
    denom_real = 1.0 + scaled
    denom_imag = -scaled
    modulus = denom_real * denom_real + denom_imag * denom_imag
    pole_real = (numer_real * denom_real + scaled * denom_imag) / modulus
    pole_imag = (scaled * denom_real - numer_real * denom_imag) / modulus
    pole_norm = pole_real * pole_real + pole_imag * pole_imag
    zero_place = 1.0 if highpass else -1.0
    section_gain = ((1.0 + zero_place * pole_real) ** 2 + pole_imag * pole_imag) / 4.0
    linear = section_gain * (2.0 * pole_real - 2.0 * zero_place)
    constant = section_gain * (1.0 - pole_norm)
    shrink = 1.0 - math.sqrt(pole_norm)
    first_out = linear / shrink
    second = (constant + pole_real * linear) / (pole_imag * shrink)
    rotation = np.array([[pole_real, -pole_imag], [pole_imag, pole_real]])
    inject = np.array([shrink, 0.0])
    return (rotation, inject, np.array([first_out, second]), section_gain)


def filter_system():
    high_rotation, high_inject, high_out, high_gain = section(low_corner, True)
    low_rotation, low_inject, low_out, low_gain = section(high_corner, False)
    upper_rows = np.concatenate([high_rotation, np.zeros((2, 2))], axis=1)
    lower_rows = np.concatenate([np.outer(low_inject, high_out), low_rotation], axis=1)
    transition = np.concatenate([upper_rows, lower_rows], axis=0)
    driving = np.concatenate([high_inject, low_inject * high_gain])
    readout = np.concatenate([high_out * low_gain, low_out])
    direct = low_gain * high_gain
    return (transition, driving, readout, direct)


def spatial_taps(extent):
    positions = np.arange(-extent, extent + 1)
    window = 0.5 * (1.0 + np.cos(np.pi * positions / (extent + 1)))
    window = window / np.sum(window)
    return np.where(positions == 0, 1.0 - window, -window)


def chain(count, power, couple):
    powers = [np.eye(4)]
    for _ in range(count):
        powers.append(powers[-1] @ power)
    ahead = np.zeros((count, 4, count, 8))
    behind = np.zeros((count, 4, count, 8))
    for at in range(count):
        for other in range(at):
            ahead[at, :, other, :4] = powers[at - 1 - other]
    for at in range(count):
        for other in range(at + 1, count):
            gives = np.einsum("pq,qjr->pjr", couple, ahead[other])
            gives[:, other, 4:] += np.eye(4)
            behind[at] += np.einsum("pq,qjr->pjr", powers[other - 1 - at], gives)
    inner = np.concatenate([ahead, behind], axis=1)
    outer = np.zeros((count, 8, 8))
    for at in range(count):
        outer[at, :4, :4] = powers[at]
    for at in range(count):
        outer[at, 4:, 4:] = powers[count - 1 - at]
        for other in range(at + 1, count):
            outer[at, 4:, :4] += powers[other - 1 - at] @ couple @ outer[other, :4, :4]
    total = np.zeros((8, count, 8))
    for other in range(count):
        total[:4, other, :4] = powers[count - 1 - other]
        gives = np.einsum("pq,qjr->pjr", couple, ahead[other])
        gives[:, other, 4:] += np.eye(4)
        total[4:] += np.einsum("pq,qjr->pjr", powers[other], gives)
    pull = sum(powers[other] @ couple @ powers[other] for other in range(count))
    return inner, outer, total, powers[count], pull


def split(table):
    high = np.asarray(table, np.float32).astype(ml_dtypes.bfloat16)
    low = (np.asarray(table, np.float64) - high.astype(np.float64)).astype(np.float32)
    return high, low.astype(ml_dtypes.bfloat16)


def thrice(table):
    high, low = split(table)
    return np.concatenate([high, high, low], axis=0)


@functools.lru_cache(maxsize=None)
def filter_tables(blocks, devices):
    transition, driving, readout, direct = filter_system()
    powers = [np.eye(4)]
    for _ in range(BLOCK):
        powers.append(powers[-1] @ transition)
    response = np.array([direct] + [readout @ powers[lag] @ driving for lag in range(BLOCK - 1)])
    lag = np.arange(BLOCK)[:, None] - np.arange(BLOCK)[None, :]
    forward = np.where(lag >= 0, response[np.clip(lag, 0, BLOCK - 1)], 0.0)
    observe = np.stack([readout @ powers[at] for at in range(BLOCK)])
    reach = np.stack([powers[BLOCK - 1 - at] @ driving for at in range(BLOCK)], axis=1)
    both_ways = forward.T @ forward
    gives = np.concatenate([reach, reach[:, ::-1] @ forward], axis=0)
    takes = np.concatenate([forward.T @ observe, observe[::-1]], axis=1)
    couple = reach[:, ::-1] @ observe
    inner, outer, total, power, pull = chain(blocks, powers[BLOCK], couple)
    across = chain(devices, power, pull)[0]
    width = 8 * blocks
    main = thrice(np.concatenate([np.tile(gives.T, (1, blocks)), both_ways], axis=1))
    correct = thrice(np.tile(takes.T, (blocks, 1)))
    outside = thrice(np.concatenate([(takes @ outer[at]).T for at in range(blocks)], axis=1))
    gathers = across.reshape(devices, 8, devices, 4, 2).transpose(0, 3, 1, 2, 4)
    return (
        main,
        np.asarray(total.reshape(8, width), np.float32),
        np.asarray(inner.reshape(width, width).T, np.float32),
        correct,
        np.asarray(gathers.reshape(devices, 32, 2 * devices), np.float32),
        outside,
    )


@functools.lru_cache(maxsize=None)
def space_tables(channels):
    taps = spatial_taps(RADIUS)

    def band(sources):
        lag = np.asarray(sources)[None, :] - np.arange(channels)[:, None] + RADIUS
        inside = (lag >= 0) & (lag <= 2 * RADIUS)
        return np.where(inside, taps[np.clip(lag, 0, 2 * RADIUS)], 0.0)

    own = band(np.arange(channels))
    edge = np.concatenate(
        [band(np.arange(-RADIUS, 0)), band(np.arange(channels, channels + RADIUS))], axis=1
    )
    parts = []
    for table in (edge, own):
        high, low = split(table)
        parts.append(np.concatenate([high, low, high], axis=1))
    states = np.zeros((channels, 3 * LANES))
    states[:, :channels] = own
    states[:, LANES : LANES + channels] = band(np.arange(-channels, 0))
    states[:, 2 * LANES : 2 * LANES + channels] = band(np.arange(channels, 2 * channels))
    return parts[0], parts[1], np.asarray(states, np.float32)


def halves(value):
    high = value.astype(jnp.bfloat16)
    return high, (value - high.astype(jnp.float32)).astype(jnp.bfloat16)


def product(left, right):
    return jnp.dot(left, right, preferred_element_type=jnp.float32)


def exact(left, right):
    return jnp.dot(left, right, precision=highest, preferred_element_type=jnp.float32)


def exact_turned(left, right):
    turned = (((1,), (1,)), ((), ()))
    return lax.dot_general(
        left, right, turned, precision=highest, preferred_element_type=jnp.float32
    )


def kernel(
    devices,
    groups,
    x_hbm,
    mask_hbm,
    main_hbm,
    total_hbm,
    inner_hbm,
    correct_hbm,
    across_hbm,
    outside_hbm,
    edge_hbm,
    own_hbm,
    states_hbm,
    out,
    x,
    mask,
    main,
    total,
    inner,
    correct,
    across,
    outside,
    edge,
    own,
    states,
    halo,
    ends,
    entering,
    load_sem,
    end_send,
    end_recv,
    near_send,
    near_recv,
    halo_send,
    halo_recv,
):
    channels, samples = x.shape
    blocks = samples // BLOCK
    width = 8 * blocks
    row, column = lax.axis_index("tm"), lax.axis_index("chan")
    below, above = lax.rem(column + groups - 1, groups), lax.rem(column + 1, groups)
    up = (above, column < groups - 1, column > 0)
    down = (below, column > 0, column < groups - 1)
    half = devices // 2
    order = sorted(range(1, devices), key=lambda step: abs(step - half))

    barrier = pltpu.get_barrier_semaphore()
    for step in order:
        peer = lax.rem(row + step, devices)
        pl.semaphore_signal(barrier, inc=1, device_id=(peer, column), device_id_type=MESH)
    for side, sends, gets in (up, down):

        @pl.when(sends)
        def _():
            pl.semaphore_signal(barrier, inc=1, device_id=(row, side), device_id_type=MESH)

    loads = []
    for index, (source, target) in enumerate(
        (
            (mask_hbm, mask),
            (x_hbm, x),
            (main_hbm, main),
            (total_hbm, total),
            (inner_hbm, inner),
            (correct_hbm, correct),
            (across_hbm.at[row], across),
            (own_hbm, own),
            (edge_hbm, edge),
            (states_hbm, states),
            (outside_hbm, outside),
        )
    ):
        copy = pltpu.make_async_copy(source, target, load_sem.at[index])
        copy.start()
        loads.append(copy)

    @pl.when(column == 0)
    def _():
        halo[pl.ds(0, RADIUS), :] = jnp.zeros((RADIUS, samples), jnp.float32)
        entering[1] = jnp.zeros((8, LANES), jnp.float32)

    @pl.when(column == groups - 1)
    def _():
        halo[pl.ds(RADIUS, RADIUS), :] = jnp.zeros((RADIUS, samples), jnp.float32)
        entering[2] = jnp.zeros((8, LANES), jnp.float32)

    loads[0].wait()
    here = lax.broadcasted_iota(jnp.int32, (channels, channels), 0)
    there = lax.broadcasted_iota(jnp.int32, (channels, channels), 1)
    live = jnp.where(here == there, mask[...].astype(jnp.float32), 0.0)
    live = jnp.sum(live, axis=1, keepdims=True)
    loads[1].wait()
    high, low = halves(
        jnp.concatenate(
            [x[:, k * BLOCK : (k + 1) * BLOCK] * live for k in range(blocks)], axis=0
        )
    )
    loads[2].wait()
    answer = product(jnp.concatenate([high, low, high], axis=1), main[...])
    slot = lax.broadcasted_iota(jnp.int32, (channels, width), 1) // 8
    given = functools.reduce(
        jnp.add,
        [
            jnp.where(slot == k, answer[k * channels : (k + 1) * channels, :width], 0.0)
            for k in range(blocks)
        ],
    )
    for load in loads[3:]:
        load.wait()
    mine = exact_turned(total[...], given)
    entering[0] = jnp.concatenate([mine, jnp.zeros((8, LANES - channels), jnp.float32)], axis=1)
    high, low = halves(exact(given, inner[...]))
    rows = []
    for k in range(blocks):
        k_high = jnp.where(slot == k, high, jnp.zeros_like(high))
        k_low = jnp.where(slot == k, low, jnp.zeros_like(low))
        rows.append(jnp.concatenate([k_high, k_low, k_high], axis=1))
    local = answer[:, width:] + product(jnp.concatenate(rows, axis=0), correct[...])
    for k in range(blocks):
        x[:, k * BLOCK : (k + 1) * BLOCK] = local[k * channels : (k + 1) * channels]

    others = jnp.where(column > 0, 1, 0) + jnp.where(column < groups - 1, 1, 0)
    pl.semaphore_wait(barrier, devices - 1 + others)

    near = []
    for way, (side, sends, gets) in enumerate((up, down)):
        copy = pltpu.make_async_remote_copy(
            src_ref=entering.at[0],
            dst_ref=entering.at[1 + way],
            send_sem=near_send.at[way],
            recv_sem=near_recv.at[way],
            device_id=(row, side),
            device_id_type=MESH,
        )
        pl.when(sends)(copy.start)
        near.append((copy, sends, gets))

    length = samples // PIECES
    pieces = []
    for piece in range(PIECES):
        span = pl.ds(piece * length, length)
        pair = []
        for way, ((side, sends, gets), source, target) in enumerate(
            ((up, channels - RADIUS, 0), (down, 0, RADIUS))
        ):
            copy = pltpu.make_async_remote_copy(
                src_ref=x.at[pl.ds(source, RADIUS), span],
                dst_ref=halo.at[pl.ds(target, RADIUS), span],
                send_sem=halo_send.at[way, piece],
                recv_sem=halo_recv.at[way, piece],
                device_id=(row, side),
                device_id_type=MESH,
            )
            pl.when(sends)(copy.start)
            pair.append((copy, sends, gets))
        pieces.append(pair)

    high, low = halves(x[...])
    out[...] = product(own[...], jnp.concatenate([high, high, low], axis=0))

    def receive(piece):
        for copy, sends, gets in pieces[piece]:
            pl.when(gets)(copy.wait_recv)
        begin, end = piece * length, (piece + 1) * length
        high, low = halves(halo[:, begin:end])
        out[:, begin:end] += product(edge[...], jnp.concatenate([high, high, low], axis=0))

    for copy, sends, gets in near:
        pl.when(gets)(copy.wait_recv)
    mine = exact_turned(
        jnp.concatenate([entering[0], entering[1], entering[2]], axis=1), states[...]
    )
    ends[row] = jnp.concatenate([mine[2 * k : 2 * k + 2] for k in range(4)], axis=1)

    def end_copy(to, slot_index):
        return pltpu.make_async_remote_copy(
            src_ref=ends.at[slot_index],
            dst_ref=ends.at[slot_index],
            send_sem=end_send.at[to],
            recv_sem=end_recv.at[slot_index],
            device_id=(to, column),
            device_id_type=MESH,
        )

    sent = []
    for step in order:
        copy = end_copy(lax.rem(row + step, devices), row)
        copy.start()
        sent.append(copy)

    for piece in range(EARLY):
        receive(piece)

    for step in reversed(order):
        end_copy(row, lax.rem(row + step, devices)).wait_recv()
    packed = jnp.concatenate([ends[k] for k in range(devices)], axis=0)
    mixed = exact(across[...], packed)
    taken = mixed[0:8, :channels] + functools.reduce(
        jnp.add,
        [
            pltpu.roll(mixed[8 * k : 8 * k + 8], LANES - 32 * k, axis=1)[:, :channels]
            for k in range(1, 4)
        ],
    )

    for piece in range(EARLY, PIECES):
        receive(piece)

    high, low = halves(taken)
    out[...] += lax.dot_general(
        jnp.concatenate([high, low, high], axis=0),
        outside[...],
        (((0,), (0,)), ((), ())),
        preferred_element_type=jnp.float32,
    )

    for copy in sent:
        copy.wait_send()
    for copy, sends, gets in near + [copy for pair in pieces for copy in pair]:
        pl.when(sends)(copy.wait_send)


def shards(devices, groups, strain, channel_mask):
    channels, samples = strain.shape
    tables = filter_tables(samples // BLOCK, devices) + space_tables(channels)
    tables = [jnp.asarray(table) for table in tables]
    f32 = jnp.float32
    held = [pltpu.VMEM(table.shape, table.dtype) for table in tables]
    held[4] = pltpu.VMEM(tables[4].shape[1:], f32)
    return pl.pallas_call(
        functools.partial(kernel, devices, groups),
        out_shape=jax.ShapeDtypeStruct((channels, samples), f32),
        in_specs=[pl.BlockSpec(memory_space=pltpu.HBM)] * (2 + len(tables)),
        out_specs=pl.BlockSpec(memory_space=pltpu.VMEM),
        scratch_shapes=[
            pltpu.VMEM((channels, samples), f32),
            pltpu.VMEM((1, channels), jnp.int32),
            *held,
            pltpu.VMEM((2 * RADIUS, samples), f32),
            pltpu.VMEM((devices, 2, LANES), f32),
            pltpu.VMEM((3, 8, LANES), f32),
            pltpu.SemaphoreType.DMA((2 + len(tables),)),
            pltpu.SemaphoreType.DMA((devices,)),
            pltpu.SemaphoreType.DMA((devices,)),
            pltpu.SemaphoreType.DMA((2,)),
            pltpu.SemaphoreType.DMA((2,)),
            pltpu.SemaphoreType.DMA((2, PIECES)),
            pltpu.SemaphoreType.DMA((2, PIECES)),
        ],
        compiler_params=pltpu.CompilerParams(
            collective_id=0, has_side_effects=True, vmem_limit_bytes=40 * 1024 * 1024
        ),
        name="bandpass",
    )(
        *[
            pltpu.with_memory_space_constraint(value, pltpu.HBM)
            for value in (strain, channel_mask.reshape(1, channels), *tables)
        ]
    )


def solution(mesh):
    placed = (P("chan", "tm"), P("chan"))
    sizes = dict(zip(mesh.axis_names, mesh.devices.shape))
    return jax.shard_map(
        functools.partial(shards, sizes["tm"], sizes["chan"]),
        mesh=mesh,
        in_specs=placed,
        out_specs=P("chan", "tm"),
        check_vma=False,
    )
```

time: 28.6 us -> 18.7 us (0.65)
  the two profiles are of different devices: /device:TPU:1 before, /device:TPU:199 now
where the time goes in v2:
time: 18.7 us; the launch traced here: 18.5 us
  Pallas kernels  17.7 us (95%)
  local copies, waits for them, and re-layouts  0.8 us (4%)
    pallas_call x1, Pallas kernels, shards(): pl.pallas_call(functools.partial(kernel, devices, groups), out_shape=jax....  17.7 us
    unnamed x1, local copies, waits for them, and re-layouts  0.8 us

profile of v2, /device:TPU:199, one launch (start us, length us, event | category | flops | bytes accessed | tf_op | source)
XLA Modules:
  0.0 18.5 jit_solution(3043506880715827963)
XLA Ops:
  0.0 17.7 %bandpass.1 = f32[32,4096]{1,0:T(8,128)S(1)} custom-call(f32[32,4096]{1,0:T(8,128)} %x_hbm.1, s32[1,32]{1,0:T(1,128)} %bitcast.1, bf16[768,384]{1,0:T(8,128)(2,1)} %constant.18.clone.main_hbm, f32[8,128]{1,0:T(8,128)} %constant.19.clone.total_hbm, f32[128,128]{1,0:T(8,128)} %constant.20.clone.inner_hbm, bf16[384,256]{1,0:T(8,128)(2,1)} %constant.21.clone.correct_hbm, ...), custom_call_target="tpu_custom_call" | custom-call | tf_op jit(solution)/shard_map/bandpass/pallas_call | solution.py:416
  17.7 0.8 %copy.13 = f32[32,4096]{1,0:T(8,128)} copy(f32[32,4096]{1,0:T(8,128)S(1)} %bandpass.1) | data formatting | bytes 1048576

commit v3 on v2

--- a/solution.py
+++ b/solution.py
@@ -14,12 +14,11 @@
 BLOCK = 256
 LANES = 128
 PIECES = 4
-EARLY = 2
+EARLY = 3
 
 low_corner = 0.015
 high_corner = 100.0
 sample_rate = 500.0
-highest = lax.Precision.HIGHEST
 MESH = pl.DeviceIdType.MESH
 
 
@@ -107,6 +106,11 @@
     return np.concatenate([high, high, low], axis=0)
 
 
+def beside(table):
+    high, low = split(table)
+    return np.concatenate([high, high, low], axis=1)
+
+
 @functools.lru_cache(maxsize=None)
 def filter_tables(blocks, devices):
     transition, driving, readout, direct = filter_system()
@@ -125,16 +129,19 @@
     inner, outer, total, power, pull = chain(blocks, powers[BLOCK], couple)
     across = chain(devices, power, pull)[0]
     width = 8 * blocks
-    main = thrice(np.concatenate([np.tile(gives.T, (1, blocks)), both_ways], axis=1))
+    first = thrice(np.tile(gives.T, (1, blocks)))
+    main = thrice(both_ways)
     correct = thrice(np.tile(takes.T, (blocks, 1)))
     outside = thrice(np.concatenate([(takes @ outer[at]).T for at in range(blocks)], axis=1))
     gathers = across.reshape(devices, 8, devices, 4, 2).transpose(0, 3, 1, 2, 4)
+    gathers = gathers.reshape(devices, 32, 2 * devices)
     return (
+        first,
+        beside(total.reshape(8, width)),
         main,
-        np.asarray(total.reshape(8, width), np.float32),
-        np.asarray(inner.reshape(width, width).T, np.float32),
+        thrice(inner.reshape(width, width).T),
         correct,
-        np.asarray(gathers.reshape(devices, 32, 2 * devices), np.float32),
+        np.stack([beside(gathers[at]) for at in range(devices)]),
         outside,
     )
 
@@ -160,7 +167,7 @@
     states[:, :channels] = own
     states[:, LANES : LANES + channels] = band(np.arange(-channels, 0))
     states[:, 2 * LANES : 2 * LANES + channels] = band(np.arange(channels, 2 * channels))
-    return parts[0], parts[1], np.asarray(states, np.float32)
+    return parts[0], parts[1], beside(states)
 
 
 def halves(value):
@@ -172,15 +179,14 @@
     return jnp.dot(left, right, preferred_element_type=jnp.float32)
 
 
-def exact(left, right):
-    return jnp.dot(left, right, precision=highest, preferred_element_type=jnp.float32)
-
-
-def exact_turned(left, right):
+def product_turned(left, right):
     turned = (((1,), (1,)), ((), ()))
-    return lax.dot_general(
-        left, right, turned, precision=highest, preferred_element_type=jnp.float32
-    )
+    return lax.dot_general(left, right, turned, preferred_element_type=jnp.float32)
+
+
+def tripled(value, axis):
+    high, low = halves(value)
+    return jnp.concatenate([high, low, high], axis=axis)
 
 
 def kernel(
@@ -188,8 +194,9 @@
     groups,
     x_hbm,
     mask_hbm,
+    first_hbm,
+    total_hbm,
     main_hbm,
-    total_hbm,
     inner_hbm,
     correct_hbm,
     across_hbm,
@@ -200,8 +207,9 @@
     out,
     x,
     mask,
+    first,
+    total,
     main,
-    total,
     inner,
     correct,
     across,
@@ -212,13 +220,16 @@
     halo,
     ends,
     entering,
+    parts,
     load_sem,
+    x_sem,
     end_send,
     end_recv,
     near_send,
     near_recv,
     halo_send,
     halo_recv,
+    relay_sem,
 ):
     channels, samples = x.shape
     blocks = samples // BLOCK
@@ -230,35 +241,49 @@
     half = devices // 2
     order = sorted(range(1, devices), key=lambda step: abs(step - half))
 
-    barrier = pltpu.get_barrier_semaphore()
-    for step in order:
-        peer = lax.rem(row + step, devices)
-        pl.semaphore_signal(barrier, inc=1, device_id=(peer, column), device_id_type=MESH)
-    for side, sends, gets in (up, down):
-
-        @pl.when(sends)
-        def _():
-            pl.semaphore_signal(barrier, inc=1, device_id=(row, side), device_id_type=MESH)
-
+    reach = -(-half // 4)
+    steps = sorted({hop % half for hop in range(-reach, reach + 1)} - {0})
+    relays = sorted({reach % half, -reach % half} - {0})
+    chip, core = row // 2, row % 2
+    greeted = [lax.rem(chip + hop, half) * 2 + core for hop in steps]
+    greeted += [lax.rem(chip + hop, half) * 2 + 1 - core for hop in [*steps, 0]]
+
+    quarter = samples // PIECES
+    arrivals = []
+    for piece in range(PIECES):
+        span = pl.ds(piece * quarter, quarter)
+        arrivals.append(pltpu.make_async_copy(x_hbm.at[:, span], x.at[:, span], x_sem.at[piece]))
     loads = []
     for index, (source, target) in enumerate(
         (
             (mask_hbm, mask),
-            (x_hbm, x),
+            (first_hbm, first),
+            (total_hbm, total),
             (main_hbm, main),
-            (total_hbm, total),
             (inner_hbm, inner),
             (correct_hbm, correct),
+            (states_hbm, states),
             (across_hbm.at[row], across),
             (own_hbm, own),
             (edge_hbm, edge),
-            (states_hbm, states),
             (outside_hbm, outside),
         )
     ):
-        copy = pltpu.make_async_copy(source, target, load_sem.at[index])
+        loads.append(pltpu.make_async_copy(source, target, load_sem.at[index]))
+    for copy in (*arrivals, *loads[:3]):
         copy.start()
-        loads.append(copy)
+
+    barrier = pltpu.get_barrier_semaphore()
+    for peer in greeted:
+        pl.semaphore_signal(barrier, inc=1, device_id=(peer, column), device_id_type=MESH)
+    for side, sends, gets in (up, down):
+
+        @pl.when(sends)
+        def _():
+            pl.semaphore_signal(barrier, inc=1, device_id=(row, side), device_id_type=MESH)
+
+    for copy in loads[3:]:
+        copy.start()
 
     @pl.when(column == 0)
     def _():
@@ -275,38 +300,50 @@
     there = lax.broadcasted_iota(jnp.int32, (channels, channels), 1)
     live = jnp.where(here == there, mask[...].astype(jnp.float32), 0.0)
     live = jnp.sum(live, axis=1, keepdims=True)
-    loads[1].wait()
-    high, low = halves(
-        jnp.concatenate(
-            [x[:, k * BLOCK : (k + 1) * BLOCK] * live for k in range(blocks)], axis=0
+    slot = lax.broadcasted_iota(jnp.int32, (channels, width), 1) // 8
+    per = quarter // BLOCK
+    given = jnp.zeros((channels, width), jnp.float32)
+    for piece in range(PIECES):
+        arrivals[piece].wait()
+        at = [(piece * per + k) * BLOCK for k in range(per)]
+        value = jnp.concatenate([x[:, k : k + BLOCK] * live for k in at], axis=0)
+        triple = tripled(value, 1)
+        size = per * channels
+        parts[piece * size : (piece + 1) * size, :] = triple
+        if piece == 0:
+            loads[1].wait()
+        answer = product(triple, first[...])
+        for k in range(per):
+            mine = answer[k * channels : (k + 1) * channels]
+            given = given + jnp.where(slot == piece * per + k, mine, 0.0)
+    given = tripled(given, 1)
+    loads[2].wait()
+    mine = product_turned(total[...], given)
+    entering[0] = jnp.concatenate([mine, jnp.zeros((8, LANES - channels), jnp.float32)], axis=1)
+
+    def finish():
+        for load in loads[3:6]:
+            load.wait()
+        high, low = halves(product(given, inner[...]))
+        rows = []
+        for k in range(blocks):
+            k_high = jnp.where(slot == k, high, jnp.zeros_like(high))
+            k_low = jnp.where(slot == k, low, jnp.zeros_like(low))
+            rows.append(jnp.concatenate([k_high, k_low, k_high], axis=1))
+        local = product(parts[...], main[...]) + product(
+            jnp.concatenate(rows, axis=0), correct[...]
         )
-    )
-    loads[2].wait()
-    answer = product(jnp.concatenate([high, low, high], axis=1), main[...])
-    slot = lax.broadcasted_iota(jnp.int32, (channels, width), 1) // 8
-    given = functools.reduce(
-        jnp.add,
-        [
-            jnp.where(slot == k, answer[k * channels : (k + 1) * channels, :width], 0.0)
-            for k in range(blocks)
-        ],
-    )
-    for load in loads[3:]:
-        load.wait()
-    mine = exact_turned(total[...], given)
-    entering[0] = jnp.concatenate([mine, jnp.zeros((8, LANES - channels), jnp.float32)], axis=1)
-    high, low = halves(exact(given, inner[...]))
-    rows = []
-    for k in range(blocks):
-        k_high = jnp.where(slot == k, high, jnp.zeros_like(high))
-        k_low = jnp.where(slot == k, low, jnp.zeros_like(low))
-        rows.append(jnp.concatenate([k_high, k_low, k_high], axis=1))
-    local = answer[:, width:] + product(jnp.concatenate(rows, axis=0), correct[...])
-    for k in range(blocks):
-        x[:, k * BLOCK : (k + 1) * BLOCK] = local[k * channels : (k + 1) * channels]
+        for k in range(blocks):
+            x[:, k * BLOCK : (k + 1) * BLOCK] = local[k * channels : (k + 1) * channels]
+
+    early = chip < half // 2
+    pl.when(early)(finish)
 
     others = jnp.where(column > 0, 1, 0) + jnp.where(column < groups - 1, 1, 0)
-    pl.semaphore_wait(barrier, devices - 1 + others)
+    pl.semaphore_wait(barrier, len(greeted) + others)
+    for hop in relays:
+        peer = lax.rem(chip + hop, half) * 2 + core
+        pl.semaphore_signal(relay_sem, inc=1, device_id=(peer, column), device_id_type=MESH)
 
     near = []
     for way, (side, sends, gets) in enumerate((up, down)):
@@ -320,6 +357,10 @@
         )
         pl.when(sends)(copy.start)
         near.append((copy, sends, gets))
+
+    pl.when(jnp.logical_not(early))(finish)
+    for load in loads[6:]:
+        load.wait()
 
     length = samples // PIECES
     pieces = []
@@ -353,8 +394,8 @@
 
     for copy, sends, gets in near:
         pl.when(gets)(copy.wait_recv)
-    mine = exact_turned(
-        jnp.concatenate([entering[0], entering[1], entering[2]], axis=1), states[...]
+    mine = product_turned(
+        tripled(jnp.concatenate([entering[0], entering[1], entering[2]], axis=1), 1), states[...]
     )
     ends[row] = jnp.concatenate([mine[2 * k : 2 * k + 2] for k in range(4)], axis=1)
 
@@ -368,6 +409,8 @@
             device_id_type=MESH,
         )
 
+    if relays:
+        pl.semaphore_wait(relay_sem, len(relays))
     sent = []
     for step in order:
         copy = end_copy(lax.rem(row + step, devices), row)
@@ -380,7 +423,7 @@
     for step in reversed(order):
         end_copy(row, lax.rem(row + step, devices)).wait_recv()
     packed = jnp.concatenate([ends[k] for k in range(devices)], axis=0)
-    mixed = exact(across[...], packed)
+    mixed = product(across[...], tripled(packed, 0))
     taken = mixed[0:8, :channels] + functools.reduce(
         jnp.add,
         [
@@ -392,9 +435,8 @@
     for piece in range(EARLY, PIECES):
         receive(piece)
 
-    high, low = halves(taken)
     out[...] += lax.dot_general(
-        jnp.concatenate([high, low, high], axis=0),
+        tripled(taken, 0),
         outside[...],
         (((0,), (0,)), ((), ())),
         preferred_element_type=jnp.float32,
@@ -412,7 +454,7 @@
     tables = [jnp.asarray(table) for table in tables]
     f32 = jnp.float32
     held = [pltpu.VMEM(table.shape, table.dtype) for table in tables]
-    held[4] = pltpu.VMEM(tables[4].shape[1:], f32)
+    held[5] = pltpu.VMEM(tables[5].shape[1:], tables[5].dtype)
     return pl.pallas_call(
         functools.partial(kernel, devices, groups),
         out_shape=jax.ShapeDtypeStruct((channels, samples), f32),
@@ -425,13 +467,16 @@
             pltpu.VMEM((2 * RADIUS, samples), f32),
             pltpu.VMEM((devices, 2, LANES), f32),
             pltpu.VMEM((3, 8, LANES), f32),
+            pltpu.VMEM((channels * samples // BLOCK, 3 * BLOCK), jnp.bfloat16),
             pltpu.SemaphoreType.DMA((2 + len(tables),)),
+            pltpu.SemaphoreType.DMA((PIECES,)),
             pltpu.SemaphoreType.DMA((devices,)),
             pltpu.SemaphoreType.DMA((devices,)),
             pltpu.SemaphoreType.DMA((2,)),
             pltpu.SemaphoreType.DMA((2,)),
             pltpu.SemaphoreType.DMA((2, PIECES)),
             pltpu.SemaphoreType.DMA((2, PIECES)),
+            pltpu.SemaphoreType.REGULAR,
         ],
         compiler_params=pltpu.CompilerParams(
             collective_id=0, has_side_effects=True, vmem_limit_bytes=40 * 1024 * 1024

time: 18.7 us -> 17.9 us (0.957)
  Pallas kernels: 17.7 us -> 16.9 us
    pallas_call x1, Pallas kernels: 17.7 us -> 16.9 us  [shards(): pl.pallas_call(functools.partial(kernel, devices, groups), out_shape=jax....]
where the time goes in v3:
time: 17.9 us; the launch traced here: 17.8 us
  Pallas kernels  16.9 us (94%)
  local copies, waits for them, and re-layouts  0.8 us (4%)
    pallas_call x1, Pallas kernels, shards(): pl.pallas_call(functools.partial(kernel, devices, groups), out_shape=jax....  16.9 us
    unnamed x1, local copies, waits for them, and re-layouts  0.8 us

profile of v3, /device:TPU:199, one launch (start us, length us, event | category | flops | bytes accessed | tf_op | source)
XLA Modules:
  0.0 17.8 jit_solution(6211395521934354426)
XLA Ops:
  0.0 16.9 %bandpass.1 = f32[32,4096]{1,0:T(8,128)S(1)} custom-call(f32[32,4096]{1,0:T(8,128)} %x_hbm.1, s32[1,32]{1,0:T(1,128)} %bitcast.1, bf16[768,128]{1,0:T(8,128)(2,1)} %constant.20.clone.first_hbm, bf16[8,384]{1,0:T(8,128)(2,1)} %constant.21.clone.total_hbm, bf16[768,256]{1,0:T(8,128)(2,1)} %constant.22.clone.main_hbm, ...), custom_call_target="tpu_custom_call" | custom-call | tf_op jit(solution)/shard_map/bandpass/pallas_call | solution.py:458
  17.0 0.8 %copy.14 = f32[32,4096]{1,0:T(8,128)} copy(f32[32,4096]{1,0:T(8,128)S(1)} %bandpass.1) | data formatting | bytes 1048576

commit v4 on v3

--- a/solution.py
+++ b/solution.py
@@ -142,6 +142,7 @@
         thrice(inner.reshape(width, width).T),
         correct,
         np.stack([beside(gathers[at]) for at in range(devices)]),
+        np.stack([beside(gathers[at][:, devices:]) for at in range(devices)]),
         outside,
     )
 
@@ -200,6 +201,7 @@
     inner_hbm,
     correct_hbm,
     across_hbm,
+    later_hbm,
     outside_hbm,
     edge_hbm,
     own_hbm,
@@ -213,6 +215,7 @@
     inner,
     correct,
     across,
+    later,
     outside,
     edge,
     own,
@@ -220,6 +223,9 @@
     halo,
     ends,
     entering,
+    straight,
+    packed_own,
+    extra,
     parts,
     load_sem,
     x_sem,
@@ -229,7 +235,10 @@
     near_recv,
     halo_send,
     halo_recv,
-    relay_sem,
+    straight_send,
+    straight_recv,
+    answer_sem,
+    slow_sem,
 ):
     channels, samples = x.shape
     blocks = samples // BLOCK
@@ -239,14 +248,38 @@
     up = (above, column < groups - 1, column > 0)
     down = (below, column > 0, column < groups - 1)
     half = devices // 2
+    quarter_rows = half // 2
+    chip, core = row // 2, row % 2
+    early = row < half
+    late = jnp.logical_not(early)
+    slow = jnp.logical_and(row == 0, column == 0)
+    quick = jnp.logical_not(slow)
+    by_slow = jnp.logical_and(row == 0, column == 1)
+    direct = jnp.logical_and(row < quarter_rows, quick)
+    first_late, last = half // 2, half - 1
+    relayed = half >= 8
+    greeters = []
+    for at in range(half):
+        before = {k for k in range(min(at, first_late))}
+        beside_it = {k for k in range(first_late, half) if at >= first_late and 0 < abs(k - at) <= 2}
+        if relayed and at == last:
+            before -= {first_late - 1}
+        greeters.append(before | beside_it)
     order = sorted(range(1, devices), key=lambda step: abs(step - half))
 
-    reach = -(-half // 4)
-    steps = sorted({hop % half for hop in range(-reach, reach + 1)} - {0})
-    relays = sorted({reach % half, -reach % half} - {0})
-    chip, core = row // 2, row % 2
-    greeted = [lax.rem(chip + hop, half) * 2 + core for hop in steps]
-    greeted += [lax.rem(chip + hop, half) * 2 + 1 - core for hop in [*steps, 0]]
+    def is_one_of(value, places):
+        return functools.reduce(jnp.logical_or, [value == place for place in places])
+
+    def pick(values):
+        return functools.reduce(
+            jnp.add, [jnp.where(chip == at, value, 0) for at, value in enumerate(values)]
+        )
+
+    columns = ((0, column, column >= 0), (1, above, column < groups - 1), (2, below, column > 0))
+
+    ends[...] = jnp.zeros_like(ends)
+    straight[...] = jnp.zeros_like(straight)
+    extra[...] = jnp.zeros_like(extra)
 
     quarter = samples // PIECES
     arrivals = []
@@ -264,6 +297,7 @@
             (correct_hbm, correct),
             (states_hbm, states),
             (across_hbm.at[row], across),
+            (later_hbm.at[row], later),
             (own_hbm, own),
             (edge_hbm, edge),
             (outside_hbm, outside),
@@ -274,16 +308,49 @@
         copy.start()
 
     barrier = pltpu.get_barrier_semaphore()
-    for peer in greeted:
-        pl.semaphore_signal(barrier, inc=1, device_id=(peer, column), device_id_type=MESH)
+
+    def greet(there, to_row, to_column):
+        @pl.when(there)
+        def _():
+            pl.semaphore_signal(
+                barrier, inc=1, device_id=(to_row, to_column), device_id_type=MESH
+            )
+
     for side, sends, gets in (up, down):
-
-        @pl.when(sends)
-        def _():
-            pl.semaphore_signal(barrier, inc=1, device_id=(row, side), device_id_type=MESH)
+        greet(jnp.logical_and(sends, quick), row, side)
+    greet(quick, chip * 2 + 1 - core, column)
+    greet(jnp.logical_and(column == 0, chip > 0), 0, 0)
+    for to in range(half):
+        sources = sorted(k for k in greeters[to])
+        if sources:
+
+            @pl.when(jnp.logical_and(is_one_of(chip, sources), quick))
+            def _():
+                for at in range(2):
+                    pl.semaphore_signal(
+                        barrier, inc=1, device_id=(2 * to + at, column), device_id_type=MESH
+                    )
+
+    @pl.when(direct)
+    def _():
+        for place, side, there in columns[1:]:
+
+            @pl.when(there)
+            def _():
+                for to in range(half, devices):
+                    pl.semaphore_signal(
+                        barrier, inc=1, device_id=(to, side), device_id_type=MESH
+                    )
 
     for copy in loads[3:]:
         copy.start()
+
+    @pl.when(slow)
+    def _():
+        pl.semaphore_wait(barrier, devices)
+        pl.semaphore_signal(slow_sem, inc=1, device_id=(0, 1), device_id_type=MESH)
+        for to in reversed(range(1, devices)):
+            pl.semaphore_signal(slow_sem, inc=1, device_id=(to, 0), device_id_type=MESH)
 
     @pl.when(column == 0)
     def _():
@@ -320,6 +387,7 @@
     loads[2].wait()
     mine = product_turned(total[...], given)
     entering[0] = jnp.concatenate([mine, jnp.zeros((8, LANES - channels), jnp.float32)], axis=1)
+    packed_own[...] = jnp.concatenate([mine[2 * k : 2 * k + 2] for k in range(4)], axis=1)
 
     def finish():
         for load in loads[3:6]:
@@ -336,14 +404,35 @@
         for k in range(blocks):
             x[:, k * BLOCK : (k + 1) * BLOCK] = local[k * channels : (k + 1) * channels]
 
-    early = chip < half // 2
-    pl.when(early)(finish)
-
     others = jnp.where(column > 0, 1, 0) + jnp.where(column < groups - 1, 1, 0)
-    pl.semaphore_wait(barrier, len(greeted) + others)
-    for hop in relays:
-        peer = lax.rem(chip + hop, half) * 2 + core
-        pl.semaphore_signal(relay_sem, inc=1, device_id=(peer, column), device_id_type=MESH)
+    greeted = pick([1 + 2 * len(sources) for sources in greeters])
+    greeted += others + jnp.where(early, 0, quarter_rows * others)
+    missed = jnp.logical_and(column == 0, is_one_of(chip, [0, *range(1, half)]))
+    missed = jnp.logical_or(missed, by_slow)
+    missed = jnp.logical_or(missed, jnp.logical_and(column == 1, late))
+
+    @pl.when(quick)
+    def _():
+        pl.semaphore_wait(barrier, greeted - jnp.where(missed, 1, 0))
+
+    answers = []
+    for to in range(first_late - 1):
+        answers.append((first_late - 1, to))
+    for to in range(first_late):
+        answers.append((last - 1 if 2 * to < first_late else first_late + 1, to))
+    if relayed:
+        answers += [(last - 1, first_late), (first_late + 1, last)]
+    for source in sorted({source for source, to in answers}):
+
+        @pl.when(chip == source)
+        def _():
+            for to in [to for source_, to in answers if source_ == source]:
+
+                @pl.when(jnp.logical_or(2 * to + core > 0, column > 0))
+                def _():
+                    pl.semaphore_signal(
+                        answer_sem, inc=1, device_id=(2 * to + core, column), device_id_type=MESH
+                    )
 
     near = []
     for way, (side, sends, gets) in enumerate((up, down)):
@@ -355,10 +444,33 @@
             device_id=(row, side),
             device_id_type=MESH,
         )
-        pl.when(sends)(copy.start)
+        now = sends if way == 0 else jnp.logical_and(sends, jnp.logical_not(by_slow))
+        pl.when(now)(copy.start)
         near.append((copy, sends, gets))
 
-    pl.when(jnp.logical_not(early))(finish)
+    def goes(place, to, there):
+        if to > 0 or place == 1:
+            return there
+        return jnp.logical_and(there, column > (0 if place == 0 else 1))
+
+    def straight_copy(place, side, to, source):
+        return pltpu.make_async_remote_copy(
+            src_ref=packed_own,
+            dst_ref=straight.at[place, source],
+            send_sem=straight_send.at[place, to],
+            recv_sem=straight_recv.at[place, source],
+            device_id=(to, side),
+            device_id_type=MESH,
+        )
+
+    @pl.when(late)
+    def _():
+        for to in range(quarter_rows):
+            for place, side, there in columns:
+                copy = straight_copy(place, side, to, row - half)
+                pl.when(goes(place, to, there))(copy.start)
+
+    finish()
     for load in loads[6:]:
         load.wait()
 
@@ -378,9 +490,17 @@
                 device_id=(row, side),
                 device_id_type=MESH,
             )
-            pl.when(sends)(copy.start)
+            now = sends if way == 0 else jnp.logical_and(sends, jnp.logical_not(by_slow))
+            pl.when(now)(copy.start)
             pair.append((copy, sends, gets))
         pieces.append(pair)
+
+    @pl.when(by_slow)
+    def _():
+        pl.semaphore_wait(slow_sem, 1)
+        near[1][0].start()
+        for pair in pieces:
+            pair[1][0].start()
 
     high, low = halves(x[...])
     out[...] = product(own[...], jnp.concatenate([high, high, low], axis=0))
@@ -409,28 +529,69 @@
             device_id_type=MESH,
         )
 
-    if relays:
-        pl.semaphore_wait(relay_sem, len(relays))
-    sent = []
+    awaited = [len([to for source, to in answers if to == at]) for at in range(half)]
+
+    @pl.when(jnp.logical_and(is_one_of(chip, [at for at in range(half) if awaited[at]]), quick))
+    def _():
+        pl.semaphore_wait(answer_sem, pick(awaited))
+
+    def to_send(step):
+        to = lax.rem(row + step, devices)
+        to_slow = jnp.logical_and(to == 0, column == 0)
+        return to, jnp.logical_and(
+            jnp.logical_or(early, to >= quarter_rows), jnp.logical_not(to_slow)
+        )
+
+    def to_get(step):
+        source = lax.rem(row + step, devices)
+        return source, jnp.logical_or(jnp.logical_not(direct), source < half)
+
     for step in order:
-        copy = end_copy(lax.rem(row + step, devices), row)
-        copy.start()
-        sent.append(copy)
+        to, there = to_send(step)
+        pl.when(there)(end_copy(to, row).start)
+
+    in_column = jnp.logical_and(column == 0, row > 0)
+
+    @pl.when(in_column)
+    def _():
+        pl.semaphore_wait(slow_sem, 1)
+        end_copy(0, row).start()
 
     for piece in range(EARLY):
         receive(piece)
 
     for step in reversed(order):
-        end_copy(row, lax.rem(row + step, devices)).wait_recv()
+        source, there = to_get(step)
+        pl.when(there)(end_copy(row, source).wait_recv)
+
+    def unpacked(value):
+        folded = [
+            pltpu.roll(value[8 * k : 8 * k + 8], LANES - 32 * k, axis=1) for k in range(1, 4)
+        ]
+        return value[0:8] + functools.reduce(jnp.add, folded)
+
+    @pl.when(direct)
+    def _():
+        for source in range(half):
+            for place, side, there in ((0, column, True), (1, below, up[2]), (2, above, down[2])):
+                copy = straight_copy(place, side, 0, source)
+                if place == 0:
+                    copy.wait_recv()
+                else:
+                    pl.when(there)(copy.wait_recv)
+        lane = lax.broadcasted_iota(jnp.int32, (8, LANES), 1)
+        gathered = []
+        for place in range(3):
+            value = jnp.concatenate([straight[place, k] for k in range(half)], axis=0)
+            value = unpacked(product(later[...], tripled(value, 0)))
+            gathered.append(jnp.where(lane < channels, value, 0.0))
+        extra[:, :channels] = product_turned(
+            tripled(jnp.concatenate(gathered, axis=1), 1), states[...]
+        )
+
     packed = jnp.concatenate([ends[k] for k in range(devices)], axis=0)
     mixed = product(across[...], tripled(packed, 0))
-    taken = mixed[0:8, :channels] + functools.reduce(
-        jnp.add,
-        [
-            pltpu.roll(mixed[8 * k : 8 * k + 8], LANES - 32 * k, axis=1)[:, :channels]
-            for k in range(1, 4)
-        ],
-    )
+    taken = (unpacked(mixed) + extra[...])[:, :channels]
 
     for piece in range(EARLY, PIECES):
         receive(piece)
@@ -442,8 +603,18 @@
         preferred_element_type=jnp.float32,
     )
 
-    for copy in sent:
-        copy.wait_send()
+    for step in order:
+        to, there = to_send(step)
+        pl.when(there)(end_copy(to, row).wait_send)
+    pl.when(in_column)(end_copy(0, row).wait_send)
+
+    @pl.when(late)
+    def _():
+        for to in range(quarter_rows):
+            for place, side, there in columns:
+                copy = straight_copy(place, side, to, row - half)
+                pl.when(goes(place, to, there))(copy.wait_send)
+
     for copy, sends, gets in near + [copy for pair in pieces for copy in pair]:
         pl.when(sends)(copy.wait_send)
 
@@ -454,7 +625,8 @@
     tables = [jnp.asarray(table) for table in tables]
     f32 = jnp.float32
     held = [pltpu.VMEM(table.shape, table.dtype) for table in tables]
-    held[5] = pltpu.VMEM(tables[5].shape[1:], tables[5].dtype)
+    for k in (5, 6):
+        held[k] = pltpu.VMEM(tables[k].shape[1:], tables[k].dtype)
     return pl.pallas_call(
         functools.partial(kernel, devices, groups),
         out_shape=jax.ShapeDtypeStruct((channels, samples), f32),
@@ -467,6 +639,9 @@
             pltpu.VMEM((2 * RADIUS, samples), f32),
             pltpu.VMEM((devices, 2, LANES), f32),
             pltpu.VMEM((3, 8, LANES), f32),
+            pltpu.VMEM((3, devices // 2, 2, LANES), f32),
+            pltpu.VMEM((2, LANES), f32),
+            pltpu.VMEM((8, LANES), f32),
             pltpu.VMEM((channels * samples // BLOCK, 3 * BLOCK), jnp.bfloat16),
             pltpu.SemaphoreType.DMA((2 + len(tables),)),
             pltpu.SemaphoreType.DMA((PIECES,)),
@@ -476,6 +651,9 @@
             pltpu.SemaphoreType.DMA((2,)),
             pltpu.SemaphoreType.DMA((2, PIECES)),
             pltpu.SemaphoreType.DMA((2, PIECES)),
+            pltpu.SemaphoreType.DMA((3, devices // 2)),
+            pltpu.SemaphoreType.DMA((3, devices // 2)),
+            pltpu.SemaphoreType.REGULAR,
             pltpu.SemaphoreType.REGULAR,
         ],
         compiler_params=pltpu.CompilerParams(

time: 17.9 us -> 16.8 us (0.939)
  the two profiles are of different devices: /device:TPU:199 before, /device:TPU:273 now
where the time goes in v4:
time: 16.8 us; the launch traced here: 16.7 us
  Pallas kernels  15.9 us (95%)
  local copies, waits for them, and re-layouts  0.8 us (5%)
    pallas_call x1, Pallas kernels, shards(): pl.pallas_call(functools.partial(kernel, devices, groups), out_shape=jax....  15.9 us
    unnamed x1, local copies, waits for them, and re-layouts  0.8 us

profile of v4, /device:TPU:273, one launch (start us, length us, event | category | flops | bytes accessed | tf_op | source)
XLA Modules:
  0.0 16.7 jit_solution(7607370730031327807)
XLA Ops:
  0.0 15.9 %bandpass.1 = f32[32,4096]{1,0:T(8,128)S(1)} custom-call(f32[32,4096]{1,0:T(8,128)} %x_hbm.1, s32[1,32]{1,0:T(1,128)} %bitcast.1, bf16[768,128]{1,0:T(8,128)(2,1)} %constant.22.clone.first_hbm, bf16[8,384]{1,0:T(8,128)(2,1)} %constant.23.clone.total_hbm, bf16[768,256]{1,0:T(8,128)(2,1)} %constant.24.clone.main_hbm, ...), custom_call_target="tpu_custom_call" | custom-call | tf_op jit(solution)/shard_map/bandpass/pallas_call | solution.py:630
  15.9 0.8 %copy.15 = f32[32,4096]{1,0:T(8,128)} copy(f32[32,4096]{1,0:T(8,128)S(1)} %bandpass.1) | data formatting | bytes 1048576

commit v5 on v4

--- a/solution.py
+++ b/solution.py
@@ -281,6 +281,18 @@
     straight[...] = jnp.zeros_like(straight)
     extra[...] = jnp.zeros_like(extra)
 
+    barrier = pltpu.get_barrier_semaphore()
+
+    def greet(there, to_row, to_column):
+        @pl.when(there)
+        def _():
+            pl.semaphore_signal(
+                barrier, inc=1, device_id=(to_row, to_column), device_id_type=MESH
+            )
+
+    for side, sends, gets in (up, down):
+        greet(jnp.logical_and(sends, quick), row, side)
+
     quarter = samples // PIECES
     arrivals = []
     for piece in range(PIECES):
@@ -307,17 +319,6 @@
     for copy in (*arrivals, *loads[:3]):
         copy.start()
 
-    barrier = pltpu.get_barrier_semaphore()
-
-    def greet(there, to_row, to_column):
-        @pl.when(there)
-        def _():
-            pl.semaphore_signal(
-                barrier, inc=1, device_id=(to_row, to_column), device_id_type=MESH
-            )
-
-    for side, sends, gets in (up, down):
-        greet(jnp.logical_and(sends, quick), row, side)
     greet(quick, chip * 2 + 1 - core, column)
     greet(jnp.logical_and(column == 0, chip > 0), 0, 0)
     for to in range(half):
@@ -389,21 +390,6 @@
     entering[0] = jnp.concatenate([mine, jnp.zeros((8, LANES - channels), jnp.float32)], axis=1)
     packed_own[...] = jnp.concatenate([mine[2 * k : 2 * k + 2] for k in range(4)], axis=1)
 
-    def finish():
-        for load in loads[3:6]:
-            load.wait()
-        high, low = halves(product(given, inner[...]))
-        rows = []
-        for k in range(blocks):
-            k_high = jnp.where(slot == k, high, jnp.zeros_like(high))
-            k_low = jnp.where(slot == k, low, jnp.zeros_like(low))
-            rows.append(jnp.concatenate([k_high, k_low, k_high], axis=1))
-        local = product(parts[...], main[...]) + product(
-            jnp.concatenate(rows, axis=0), correct[...]
-        )
-        for k in range(blocks):
-            x[:, k * BLOCK : (k + 1) * BLOCK] = local[k * channels : (k + 1) * channels]
-
     others = jnp.where(column > 0, 1, 0) + jnp.where(column < groups - 1, 1, 0)
     greeted = pick([1 + 2 * len(sources) for sources in greeters])
     greeted += others + jnp.where(early, 0, quarter_rows * others)
@@ -470,13 +456,24 @@
                 copy = straight_copy(place, side, to, row - half)
                 pl.when(goes(place, to, there))(copy.start)
 
-    finish()
-    for load in loads[6:]:
+    for load in loads[3:6]:
         load.wait()
-
+    high, low = halves(product(given, inner[...]))
     length = samples // PIECES
     pieces = []
     for piece in range(PIECES):
+        rows = []
+        for k in range(piece * per, (piece + 1) * per):
+            k_high = jnp.where(slot == k, high, jnp.zeros_like(high))
+            k_low = jnp.where(slot == k, low, jnp.zeros_like(low))
+            rows.append(jnp.concatenate([k_high, k_low, k_high], axis=1))
+        size = per * channels
+        local = product(parts[piece * size : (piece + 1) * size, :], main[...]) + product(
+            jnp.concatenate(rows, axis=0), correct[...]
+        )
+        for k in range(per):
+            at = piece * length + k * BLOCK
+            x[:, at : at + BLOCK] = local[k * channels : (k + 1) * channels]
         span = pl.ds(piece * length, length)
         pair = []
         for way, ((side, sends, gets), source, target) in enumerate(
@@ -494,6 +491,8 @@
             pl.when(now)(copy.start)
             pair.append((copy, sends, gets))
         pieces.append(pair)
+    for load in loads[6:]:
+        load.wait()
 
     @pl.when(by_slow)
     def _():
@@ -559,6 +558,21 @@
 
     for piece in range(EARLY):
         receive(piece)
+
+    for step in order:
+        to, there = to_send(step)
+        pl.when(there)(end_copy(to, row).wait_send)
+    pl.when(in_column)(end_copy(0, row).wait_send)
+
+    @pl.when(late)
+    def _():
+        for to in range(quarter_rows):
+            for place, side, there in columns:
+                copy = straight_copy(place, side, to, row - half)
+                pl.when(goes(place, to, there))(copy.wait_send)
+
+    for copy, sends, gets in near + [copy for pair in pieces[:-1] for copy in pair]:
+        pl.when(sends)(copy.wait_send)
 
     for step in reversed(order):
         source, there = to_get(step)
@@ -603,19 +617,7 @@
         preferred_element_type=jnp.float32,
     )
 
-    for step in order:
-        to, there = to_send(step)
-        pl.when(there)(end_copy(to, row).wait_send)
-    pl.when(in_column)(end_copy(0, row).wait_send)
-
-    @pl.when(late)
-    def _():
-        for to in range(quarter_rows):
-            for place, side, there in columns:
-                copy = straight_copy(place, side, to, row - half)
-                pl.when(goes(place, to, there))(copy.wait_send)
-
-    for copy, sends, gets in near + [copy for pair in pieces for copy in pair]:
+    for copy, sends, gets in pieces[-1]:
         pl.when(sends)(copy.wait_send)
 
 

time: 16.8 us -> 16.8 us (level)
  no operation moved by 1% of the time
where the time goes in v5:
time: 16.8 us; the launch traced here: 16.7 us
  Pallas kernels  15.9 us (95%)
  local copies, waits for them, and re-layouts  0.8 us (5%)
    pallas_call x1, Pallas kernels, shards(): pl.pallas_call(functools.partial(kernel, devices, groups), out_shape=jax....  15.9 us
    unnamed x1, local copies, waits for them, and re-layouts  0.8 us

profile of v5, /device:TPU:273, one launch (start us, length us, event | category | flops | bytes accessed | tf_op | source)
XLA Modules:
  0.0 16.7 jit_solution(7403889165304708945)
XLA Ops:
  0.0 15.9 %bandpass.1 = f32[32,4096]{1,0:T(8,128)S(1)} custom-call(f32[32,4096]{1,0:T(8,128)} %x_hbm.1, s32[1,32]{1,0:T(1,128)} %bitcast.1, bf16[768,128]{1,0:T(8,128)(2,1)} %constant.22.clone.first_hbm, bf16[8,384]{1,0:T(8,128)(2,1)} %constant.23.clone.total_hbm, bf16[768,256]{1,0:T(8,128)(2,1)} %constant.24.clone.main_hbm, ...), custom_call_target="tpu_custom_call" | custom-call | tf_op jit(solution)/shard_map/bandpass/pallas_call | solution.py:632
  15.9 0.8 %copy.15 = f32[32,4096]{1,0:T(8,128)} copy(f32[32,4096]{1,0:T(8,128)S(1)} %bandpass.1) | data formatting | bytes 1048576

commit v6 on v5

--- a/solution.py
+++ b/solution.py
@@ -13,8 +13,8 @@
 RADIUS = 16
 BLOCK = 256
 LANES = 128
-PIECES = 4
-EARLY = 3
+PIECES = 2
+EARLY = 1
 
 low_corner = 0.015
 high_corner = 100.0

time: 16.8 us -> 16.7 us (level)
  no operation moved by 1% of the time
where the time goes in v6:
time: 16.7 us; the launch traced here: 16.6 us
  Pallas kernels  15.8 us (95%)
  local copies, waits for them, and re-layouts  0.8 us (5%)
    pallas_call x1, Pallas kernels, shards(): pl.pallas_call(functools.partial(kernel, devices, groups), out_shape=jax....  15.8 us
    unnamed x1, local copies, waits for them, and re-layouts  0.8 us

profile of v6, /device:TPU:273, one launch (start us, length us, event | category | flops | bytes accessed | tf_op | source)
XLA Modules:
  0.0 16.6 jit_solution(12202166082134589658)
XLA Ops:
  0.0 15.8 %bandpass.1 = f32[32,4096]{1,0:T(8,128)S(1)} custom-call(f32[32,4096]{1,0:T(8,128)} %x_hbm.1, s32[1,32]{1,0:T(1,128)} %bitcast.1, bf16[768,128]{1,0:T(8,128)(2,1)} %constant.22.clone.first_hbm, bf16[8,384]{1,0:T(8,128)(2,1)} %constant.23.clone.total_hbm, bf16[768,256]{1,0:T(8,128)(2,1)} %constant.24.clone.main_hbm, ...), custom_call_target="tpu_custom_call" | custom-call | tf_op jit(solution)/shard_map/bandpass/pallas_call | solution.py:632
  15.8 0.8 %copy.15 = f32[32,4096]{1,0:T(8,128)} copy(f32[32,4096]{1,0:T(8,128)S(1)} %bandpass.1) | data formatting | bytes 1048576

commit v7 on v6

--- a/solution.py
+++ b/solution.py
@@ -14,6 +14,7 @@
 BLOCK = 256
 LANES = 128
 PIECES = 2
+LOADS = 4
 EARLY = 1
 
 low_corner = 0.015
@@ -293,9 +294,9 @@
     for side, sends, gets in (up, down):
         greet(jnp.logical_and(sends, quick), row, side)
 
-    quarter = samples // PIECES
+    quarter = samples // LOADS
     arrivals = []
-    for piece in range(PIECES):
+    for piece in range(LOADS):
         span = pl.ds(piece * quarter, quarter)
         arrivals.append(pltpu.make_async_copy(x_hbm.at[:, span], x.at[:, span], x_sem.at[piece]))
     loads = []
@@ -371,7 +372,7 @@
     slot = lax.broadcasted_iota(jnp.int32, (channels, width), 1) // 8
     per = quarter // BLOCK
     given = jnp.zeros((channels, width), jnp.float32)
-    for piece in range(PIECES):
+    for piece in range(LOADS):
         arrivals[piece].wait()
         at = [(piece * per + k) * BLOCK for k in range(per)]
         value = jnp.concatenate([x[:, k : k + BLOCK] * live for k in at], axis=0)
@@ -460,6 +461,7 @@
         load.wait()
     high, low = halves(product(given, inner[...]))
     length = samples // PIECES
+    per = length // BLOCK
     pieces = []
     for piece in range(PIECES):
         rows = []
@@ -646,7 +648,7 @@
             pltpu.VMEM((8, LANES), f32),
             pltpu.VMEM((channels * samples // BLOCK, 3 * BLOCK), jnp.bfloat16),
             pltpu.SemaphoreType.DMA((2 + len(tables),)),
-            pltpu.SemaphoreType.DMA((PIECES,)),
+            pltpu.SemaphoreType.DMA((LOADS,)),
             pltpu.SemaphoreType.DMA((devices,)),
             pltpu.SemaphoreType.DMA((devices,)),
             pltpu.SemaphoreType.DMA((2,)),

time: 16.7 us -> 16.7 us (level)
  no operation moved by 1% of the time
where the time goes in v7:
time: 16.7 us; the launch traced here: 16.6 us
  Pallas kernels  15.8 us (95%)
  local copies, waits for them, and re-layouts  0.8 us (5%)
    pallas_call x1, Pallas kernels, shards(): pl.pallas_call(functools.partial(kernel, devices, groups), out_shape=jax....  15.8 us
    unnamed x1, local copies, waits for them, and re-layouts  0.8 us

profile of v7, /device:TPU:273, one launch (start us, length us, event | category | flops | bytes accessed | tf_op | source)
XLA Modules:
  0.0 16.6 jit_solution(18087803171752132330)
XLA Ops:
  0.0 15.8 %bandpass.1 = f32[32,4096]{1,0:T(8,128)S(1)} custom-call(f32[32,4096]{1,0:T(8,128)} %x_hbm.1, s32[1,32]{1,0:T(1,128)} %bitcast.1, bf16[768,128]{1,0:T(8,128)(2,1)} %constant.22.clone.first_hbm, bf16[8,384]{1,0:T(8,128)(2,1)} %constant.23.clone.total_hbm, bf16[768,256]{1,0:T(8,128)(2,1)} %constant.24.clone.main_hbm, ...), custom_call_target="tpu_custom_call" | custom-call | tf_op jit(solution)/shard_map/bandpass/pallas_call | solution.py:634
  15.8 0.8 %copy.15 = f32[32,4096]{1,0:T(8,128)} copy(f32[32,4096]{1,0:T(8,128)S(1)} %bandpass.1) | data formatting | bytes 1048576
